TPU v7x, 512 devices: a whole 4x4x16 slice. The times are simulated.
512 devices in a mesh: sx: 4 (over y), sy: 8 (over z_lo, core), sz: 16 (over x, z_hi).
Axes of the slice: x: 4, y: 4, z: 16 (z_hi: 4, z_lo: 4; z = z_hi * 4 + z_lo), core: 2. Of those that a mesh axis runs over, the one named last changes fastest.
Arguments:
- density: bfloat16 [4, 32, 64, 256], P(None, 'sx', 'sy', 'sz'), may hold values from -6 to 6
- conv1_weight: bfloat16 [32, 3, 3, 3, 4], replicated, may hold values from -0.625 to 0.625
- conv1_bias: float32 [32], replicated, may hold values from -3 to 3
- conv1_probe: bfloat16 [32, 3, 3, 3, 4], replicated, may hold values from -0.625 to 0.625
- conv2_weight: bfloat16 [32, 3, 3, 3, 32], replicated, may hold values from -0.21875 to 0.21875
- conv2_bias: float32 [32], replicated, may hold values from -3 to 3
- conv2_probe: bfloat16 [32, 3, 3, 3, 32], replicated, may hold values from -0.21875 to 0.21875
- lift_weight: bfloat16 [256, 4, 4, 4, 32], replicated, may hold values from -0.125 to 0.125
- lift_bias: float32 [256], replicated, may hold values from -3 to 3
- lift_probe: bfloat16 [256, 4, 4, 4, 32], replicated, may hold values from -0.125 to 0.125
- conv3_weight: bfloat16 [256, 3, 3, 3, 256], P(None, None, None, None, ('sx', 'sy')), may hold values from -0.125 to 0.125
- conv3_bias: float32 [256], P(('sx', 'sy')), may hold values from -3 to 3
- conv3_probe: bfloat16 [256, 3, 3, 3, 256], P(None, None, None, None, ('sx', 'sy')), may hold values from -0.125 to 0.125
Outputs:
- features: bfloat16 [256, 8, 16, 64], P(('sx', 'sy'), None, None, 'sz')
- tangent: bfloat16 [256, 8, 16, 64], P(('sx', 'sy'), None, None, 'sz')
All inputs are finite; a program needn't handle non-finite values.
Results may differ from a plain program's by a relative error of at most 0.013.
Values may be sent and summed in bfloat16 or wider, within the bound.
No kernel may reach another device: no remote copies, remote signals or barrier semaphores. Data moves between devices by JAX's collectives and lax.ppermute only.
A program may use at most 64 MiB of HBM per device.

v0:
```python
import jax
import jax.numpy as jnp
from jax import lax
from jax.sharding import PartitionSpec as P


def with_halo(cells, sides, width):
    for axis, dim in sides:
        count = lax.axis_size(axis)
        ends = count - 1
        head = lax.slice_in_dim(cells, 0, width, axis=dim)
        tail = lax.slice_in_dim(cells, cells.shape[dim] - width, cells.shape[dim], axis=dim)
        cells = jnp.concatenate(
            [
                lax.ppermute(tail, axis, [(i, (i + 1) % count) for i in range(ends)]),
                cells,
                lax.ppermute(head, axis, [((i + 1) % count, i) for i in range(ends)]),
            ],
            axis=dim,
        )
    return cells


def swish_pair(preact, direction):
    sigmoid_value = jax.nn.sigmoid(preact)
    derivative = sigmoid_value * (1.0 + preact * (1.0 - sigmoid_value))
    return (preact * sigmoid_value, derivative * direction)


def cells(volume, weight, stride, out_order):
    return lax.conv_general_dilated(
        volume,
        weight,
        (stride, stride, stride),
        "VALID",
        dimension_numbers=("NCDHW", "ODHWI", out_order),
        preferred_element_type=jnp.float32,
    )


def per_channel(vector):
    return vector[:, None, None, None]


def body(
    density,
    conv1_weight,
    conv1_bias,
    conv1_probe,
    conv2_weight,
    conv2_bias,
    conv2_probe,
    lift_weight,
    lift_bias,
    lift_probe,
    conv3_weight,
    conv3_bias,
    conv3_probe,
):
    width_one = conv1_weight.shape[0]
    width_three = lift_weight.shape[0]
    both_first = jnp.concatenate([conv1_weight, conv1_probe], 0)
    padded = with_halo(density, (("sx", 1), ("sy", 2), ("sz", 3)), 1)
    pre_both = cells(padded[None], both_first, 1, "NCDHW")[0]
    hidden, probe = swish_pair(pre_both[:width_one] + per_channel(conv1_bias), pre_both[width_one:])
    stacked = jnp.stack([hidden.astype(jnp.bfloat16), probe.astype(jnp.bfloat16)])
    pair = with_halo(stacked, (("sx", 2), ("sy", 3), ("sz", 4)), 1)
    both = cells(pair, conv2_weight, 1, "NCDHW")
    extra = cells(pair[:1], conv2_probe, 1, "NCDHW")[0]
    hidden, probe = swish_pair(both[0] + per_channel(conv2_bias), both[1] + extra)
    pair = jnp.stack([hidden.astype(jnp.bfloat16), probe.astype(jnp.bfloat16)])
    both = cells(pair, lift_weight, 4, "NCDHW")
    extra = cells(pair[:1], lift_probe, 4, "NCDHW")[0]
    hidden, probe = swish_pair(both[0] + per_channel(lift_bias), both[1] + extra)
    stacked = jnp.stack([hidden.astype(jnp.bfloat16), probe.astype(jnp.bfloat16)])
    coarse_x, coarse_y, coarse_z = (stacked.shape[2], stacked.shape[3], stacked.shape[4])
    across = lax.axis_size("sx")
    downward = lax.axis_size("sy")
    per_device = width_three // (across * downward)
    rimmed = with_halo(stacked, (("sx", 2), ("sy", 3), ("sz", 4)), 1)
    zero_sums = jnp.zeros((width_three, coarse_x, coarse_y, coarse_z), jnp.float32)
    pieces = (
        lax.all_gather(conv3_weight, ("sx", "sy"), axis=4, tiled=True),
        lax.all_gather(conv3_probe, ("sx", "sy"), axis=4, tiled=True),
    )
    piece_count = pieces[0].shape[4]
    channel_block = lax.slice_in_dim(rimmed, 0, piece_count, axis=1)
    pair_sums = cells(channel_block, pieces[0], 1, "NCDHW")
    probe_sums = cells(channel_block[:1], pieces[1], 1, "NCDHW")[0]
    primal_sum = zero_sums + pair_sums[0]
    change_sum = zero_sums + pair_sums[1] + probe_sums
    totals = jnp.stack([primal_sum, change_sum]).reshape(
        2, across, downward, per_device, coarse_x, coarse_y, coarse_z
    )
    received = lax.all_to_all(
        lax.all_to_all(totals.astype(jnp.bfloat16), "sx", split_axis=1, concat_axis=4, tiled=True),
        "sy",
        split_axis=2,
        concat_axis=5,
        tiled=True,
    ).astype(totals.dtype)
    primal = received[0, 0, 0]
    change = received[1, 0, 0]
    features = (primal + per_channel(conv3_bias)).astype(jnp.bfloat16)
    return (features, change.astype(jnp.bfloat16))


def solution(mesh):
    placed = (
        P(None, "sx", "sy", "sz"),
        P(),
        P(),
        P(),
        P(),
        P(),
        P(),
        P(),
        P(),
        P(),
        P(None, None, None, None, ("sx", "sy")),
        P(("sx", "sy")),
        P(None, None, None, None, ("sx", "sy")),
    )
    return jax.shard_map(
        body,
        mesh=mesh,
        in_specs=placed,
        out_specs=(P(("sx", "sy"), None, None, "sz"), P(("sx", "sy"), None, None, "sz")),
        check_vma=False,
    )
```

profile of v0, /device:TPU:6, one launch (start us, length us, event | category | flops | bytes accessed | tf_op | source)
XLA Modules:
  0.0 209.7 jit_solution(18133274675240034810)
XLA Ops:
  8.0 0.7 fusion.54
  8.7 3.5 %collective-permute-start = (bf16[4,1,8,16]{3,2,1,0:T(8,128)(2,1)S(1)}, bf16[4,1,8,16]{3,2,1,0:T(8,128)(2,1)S(1)}, u32[]{:S(2)}, u32[]{:S(2)}) collective-permute-start(bf16[4,1,8,16]{3,2,1,0:T(8,128)(2,1)S(1)} %get-tuple-element.29), channel_id=1, source_target_pairs={{0,128},{128,256},{256,384},{1,129},{129,257},{257,385},{2,130},{1... | collective-permute-start | bytes 3080 | tf_op jit(solution)/shard_map/ppermute | solution.py:15
  12.2 1.3 collective-permute-start.1
  13.5 0.9 constant_dynamic-update-slice_fusion.1
  14.4 3.3 %collective-permute-done.1 = bf16[4,1,8,16]{3,2,1,0:T(8,128)(2,1)S(1)} collective-permute-done((bf16[4,1,8,16]{3,2,1,0:T(8,128)(2,1)S(1)}, bf16[4,1,8,16]{3,2,1,0:T(8,128)(2,1)S(1)}, u32[]{:S(2)}, u32[]{:S(2)}) %collective-permute-start.1) | collective-permute-done | bytes 1056 | tf_op jit(solution)/shard_map/ppermute | solution.py:17
  17.8 1.3 collective-permute-start.2
  19.1 1.3 collective-permute-start.3
  20.4 3.9 %collective-permute-done.3 = bf16[4,10,1,16]{3,2,1,0:T(2,128)(2,1)S(1)} collective-permute-done((bf16[4,10,1,16]{3,2,1,0:T(2,128)(2,1)S(1)}, bf16[4,10,1,16]{3,2,1,0:T(2,128)(2,1)S(1)}, u32[]{:S(2)}, u32[]{:S(2)}) %collective-permute-start.3) | collective-permute-done | bytes 1312 | tf_op jit(solution)/shard_map/ppermute | solution.py:17
  24.5 9.1 %collective-permute-start.4 = (bf16[4,10,10,1]{3,2,1,0:T(8,128)(2,1)S(1)}, bf16[4,10,10,1]{3,2,1,0:T(8,128)(2,1)S(1)}, u32[]{:S(2)}, u32[]{:S(2)}) collective-permute-start(bf16[4,10,10,1]{3,2,1,0:T(8,128)(2,1)S(1)} %get-tuple-element.22), channel_id=1, source_target_pairs={{0,1},{1,2},{2,3},{3,4},{4,5},{5,6},{6,7},{7,8},{8,9},{9,10},{10,1... | collective-permute-start | bytes 2408 | tf_op jit(solution)/shard_map/ppermute | solution.py:15
  33.6 4.9 %collective-permute-start.5 = (bf16[4,10,10,1]{3,2,1,0:T(8,128)(2,1)S(1)}, bf16[4,10,10,1]{3,2,1,0:T(8,128)(2,1)S(1)}, u32[]{:S(2)}, u32[]{:S(2)}) collective-permute-start(bf16[4,10,10,1]{3,2,1,0:T(8,128)(2,1)S(1)} %get-tuple-element.23), channel_id=1, source_target_pairs={{1,0},{2,1},{3,2},{4,3},{5,4},{6,5},{7,6},{8,7},{9,8},{10,9},{11,1... | collective-permute-start | bytes 2408 | tf_op jit(solution)/shard_map/ppermute | solution.py:17
  38.6 8.5 %collective-permute-done.4 = bf16[4,10,10,1]{3,2,1,0:T(8,128)(2,1)S(1)} collective-permute-done((bf16[4,10,10,1]{3,2,1,0:T(8,128)(2,1)S(1)}, bf16[4,10,10,1]{3,2,1,0:T(8,128)(2,1)S(1)}, u32[]{:S(2)}, u32[]{:S(2)}) %collective-permute-start.4) | collective-permute-done | bytes 832 | tf_op jit(solution)/shard_map/ppermute | solution.py:15
  47.1 3.6 %collective-permute-done.5 = bf16[4,10,10,1]{3,2,1,0:T(8,128)(2,1)S(1)} collective-permute-done((bf16[4,10,10,1]{3,2,1,0:T(8,128)(2,1)S(1)}, bf16[4,10,10,1]{3,2,1,0:T(8,128)(2,1)S(1)}, u32[]{:S(2)}, u32[]{:S(2)}) %collective-permute-start.5) | collective-permute-done | bytes 832 | tf_op jit(solution)/shard_map/ppermute | solution.py:17
  51.5 0.8 copy.57
  52.6 1.8 convolution_select_fusion.1
  55.0 6.8 %collective-permute-start.6 = (bf16[2,32,1,8,16]{1,3,4,2,0:T(8,128)(2,1)S(1)}, bf16[2,32,1,8,16]{1,3,4,2,0:T(8,128)(2,1)S(1)}, u32[]{:S(2)}, u32[]{:S(2)}) collective-permute-start(bf16[2,32,1,8,16]{1,3,4,2,0:T(8,128)(2,1)S(1)} %get-tuple-element.18), channel_id=1, source_target_pairs={{0,128},{128,256},{256,384},{1,129},{129,257},{257,385},{2,130},{1... | collective-permute-start | bytes 49160 | tf_op jit(solution)/shard_map/ppermute | solution.py:15
  61.7 1.3 collective-permute-start.7
  63.6 4.8 %collective-permute-done.7 = bf16[2,32,1,8,16]{1,3,4,2,0:T(8,128)(2,1)S(1)} collective-permute-done((bf16[2,32,1,8,16]{1,3,4,2,0:T(8,128)(2,1)S(1)}, bf16[2,32,1,8,16]{1,3,4,2,0:T(8,128)(2,1)S(1)}, u32[]{:S(2)}, u32[]{:S(2)}) %collective-permute-start.7) | collective-permute-done | bytes 16416 | tf_op jit(solution)/shard_map/ppermute | solution.py:17
  68.6 3.7 %collective-permute-start.8 = (bf16[2,32,10,1,16]{1,3,4,2,0:T(2,128)(2,1)S(1)}, bf16[2,32,10,1,16]{1,3,4,2,0:T(2,128)(2,1)S(1)}, u32[]{:S(2)}, u32[]{:S(2)}) collective-permute-start(bf16[2,32,10,1,16]{1,3,4,2,0:T(2,128)(2,1)S(1)} %get-tuple-element.16), channel_id=1, source_target_pairs={{0,16},{16,32},{32,48},{48,64},{64,80},{80,96},{96,112},{1,17},{17... | collective-permute-start | bytes 61448 | tf_op jit(solution)/shard_map/ppermute | solution.py:15
  72.3 1.3 collective-permute-start.9
  73.6 4.8 %collective-permute-done.9 = bf16[2,32,10,1,16]{1,3,4,2,0:T(2,128)(2,1)S(1)} collective-permute-done((bf16[2,32,10,1,16]{1,3,4,2,0:T(2,128)(2,1)S(1)}, bf16[2,32,10,1,16]{1,3,4,2,0:T(2,128)(2,1)S(1)}, u32[]{:S(2)}, u32[]{:S(2)}) %collective-permute-start.9) | collective-permute-done | bytes 20512 | tf_op jit(solution)/shard_map/ppermute | solution.py:17
  78.6 6.8 %collective-permute-start.10 = (bf16[2,32,10,10,1]{1,3,4,2,0:T(8,128)(2,1)S(1)}, bf16[2,32,10,10,1]{1,3,4,2,0:T(8,128)(2,1)S(1)}, u32[]{:S(2)}, u32[]{:S(2)}) collective-permute-start(bf16[2,32,10,10,1]{1,3,4,2,0:T(8,128)(2,1)S(1)} %get-tuple-element.12), channel_id=1, source_target_pairs={{0,1},{1,2},{2,3},{3,4},{4,5},{5,6},{6,7},{7,8},{8,9},{9,10},{10,1... | collective-permute-start | bytes 38408 | tf_op jit(solution)/shard_map/ppermute | solution.py:15
  85.3 4.1 %collective-permute-start.11 = (bf16[2,32,10,10,1]{1,3,4,2,0:T(8,128)(2,1)S(1)}, bf16[2,32,10,10,1]{1,3,4,2,0:T(8,128)(2,1)S(1)}, u32[]{:S(2)}, u32[]{:S(2)}) collective-permute-start(bf16[2,32,10,10,1]{1,3,4,2,0:T(8,128)(2,1)S(1)} %get-tuple-element.13), channel_id=1, source_target_pairs={{1,0},{2,1},{3,2},{4,3},{5,4},{6,5},{7,6},{8,7},{9,8},{10,9},{11,1... | collective-permute-start | bytes 38408 | tf_op jit(solution)/shard_map/ppermute | solution.py:17
  90.0 5.8 %collective-permute-done.11 = bf16[2,32,10,10,1]{1,3,4,2,0:T(8,128)(2,1)S(1)} collective-permute-done((bf16[2,32,10,10,1]{1,3,4,2,0:T(8,128)(2,1)S(1)}, bf16[2,32,10,10,1]{1,3,4,2,0:T(8,128)(2,1)S(1)}, u32[]{:S(2)}, u32[]{:S(2)}) %collective-permute-start.11) | collective-permute-done | bytes 12832 | tf_op jit(solution)/shard_map/ppermute | solution.py:17
  95.8 1.4 pad_maximum_fusion
  98.3 1.4 convolution_select_fusion
  99.8 1.4 fusion.63
  101.3 0.9 copy.91
  102.2 1.1 pad.2.clone
  103.9 2.4 %fusion = bf16[32,10,10,2,8,5]{0,3,5,4,2,1:T(2,128)(2,1)S(1)} fusion(bf16[32,10,10,2,7,2]{0,3,5,4,2,1:T(2,128)(2,1)S(1)} %slice.145, bf16[32,10,10,2,8,3]{0,3,5,4,2,1:T(2,128)(2,1)S(1)} %bitcast.66), kind=kLoop, calls=%fused_computation.1 | loop fusion | flops 1536000 | bytes 998400 | tf_op jit(solution)/shard_map/conv_general_dilated | solution.py:31
  106.3 2.3 %fusion.5 = f32[8,8,16,3,32]{4,2,3,1,0:T(8,128)S(1)} fusion(bf16[32,3,3,3,32]{4,0,3,2,1:T(8,128)(2,1)S(1)} %copy-done.7, bf16[32,10,10,2,8,5]{0,3,5,4,2,1:T(2,128)(2,1)S(1)} %fusion, pred[16,3]{0,1:T(4,128)(4,1)S(1)} %copy-done.10), kind=kOutput, calls=%fused_computation.8 | convolution fusion | flops 169967616 | bytes 960560 | tf_op jit(solution)/shard_map/conv_general_dilated | solution.py:31
  110.3 1.1 fusion.18
  111.4 0.8 fusion.20
  112.4 5.5 %collective-permute-start.12 = (bf16[2,256,1,2,4]{1,4,3,2,0:T(4,128)(2,1)S(1)}, bf16[2,256,1,2,4]{1,4,3,2,0:T(4,128)(2,1)S(1)}, u32[]{:S(2)}, u32[]{:S(2)}) collective-permute-start(bf16[2,256,1,2,4]{1,4,3,2,0:T(4,128)(2,1)S(1)} %get-tuple-element.36), channel_id=1, source_target_pairs={{0,128},{128,256},{256,384},{1,129},{129,257},{257,385},{2,130},{1... | collective-permute-start | bytes 24584 | tf_op jit(solution)/shard_map/ppermute | solution.py:15
  117.9 1.3 collective-permute-start.13
  119.2 4.2 %collective-permute-done.13 = bf16[2,256,1,2,4]{1,4,3,2,0:T(4,128)(2,1)S(1)} collective-permute-done((bf16[2,256,1,2,4]{1,4,3,2,0:T(4,128)(2,1)S(1)}, bf16[2,256,1,2,4]{1,4,3,2,0:T(4,128)(2,1)S(1)}, u32[]{:S(2)}, u32[]{:S(2)}) %collective-permute-start.13) | collective-permute-done | bytes 8224 | tf_op jit(solution)/shard_map/ppermute | solution.py:17
  123.5 4.8 %collective-permute-start.14 = (bf16[2,256,4,1,4]{1,4,3,2,0:T(4,128)(2,1)S(1)}, bf16[2,256,4,1,4]{1,4,3,2,0:T(4,128)(2,1)S(1)}, u32[]{:S(2)}, u32[]{:S(2)}) collective-permute-start(bf16[2,256,4,1,4]{1,4,3,2,0:T(4,128)(2,1)S(1)} %get-tuple-element.30), channel_id=1, source_target_pairs={{0,16},{16,32},{32,48},{48,64},{64,80},{80,96},{96,112},{1,17},{17... | collective-permute-start | bytes 49160 | tf_op jit(solution)/shard_map/ppermute | solution.py:15
  128.3 1.3 collective-permute-start.15
  129.6 2.8 %collective-permute-done.15 = bf16[2,256,4,1,4]{1,4,3,2,0:T(4,128)(2,1)S(1)} collective-permute-done((bf16[2,256,4,1,4]{1,4,3,2,0:T(4,128)(2,1)S(1)}, bf16[2,256,4,1,4]{1,4,3,2,0:T(4,128)(2,1)S(1)}, u32[]{:S(2)}, u32[]{:S(2)}) %collective-permute-start.15) | collective-permute-done | bytes 16416 | tf_op jit(solution)/shard_map/ppermute | solution.py:17
  132.5 5.0 %collective-permute-start.16 = (bf16[2,256,4,4,1]{1,4,3,2,0:T(2,128)(2,1)S(1)}, bf16[2,256,4,4,1]{1,4,3,2,0:T(2,128)(2,1)S(1)}, u32[]{:S(2)}, u32[]{:S(2)}) collective-permute-start(bf16[2,256,4,4,1]{1,4,3,2,0:T(2,128)(2,1)S(1)} %get-tuple-element.26), channel_id=1, source_target_pairs={{0,1},{1,2},{2,3},{3,4},{4,5},{5,6},{6,7},{7,8},{8,9},{9,10},{10,1... | collective-permute-start | bytes 49160 | tf_op jit(solution)/shard_map/ppermute | solution.py:15
  137.5 5.7 %collective-permute-start.17 = (bf16[2,256,4,4,1]{1,4,3,2,0:T(2,128)(2,1)S(1)}, bf16[2,256,4,4,1]{1,4,3,2,0:T(2,128)(2,1)S(1)}, u32[]{:S(2)}, u32[]{:S(2)}) collective-permute-start(bf16[2,256,4,4,1]{1,4,3,2,0:T(2,128)(2,1)S(1)} %get-tuple-element.27), channel_id=1, source_target_pairs={{1,0},{2,1},{3,2},{4,3},{5,4},{6,5},{7,6},{8,7},{9,8},{10,9},{11,1... | collective-permute-start | bytes 49160 | tf_op jit(solution)/shard_map/ppermute | solution.py:17
  143.2 4.1 %collective-permute-done.17 = bf16[2,256,4,4,1]{1,4,3,2,0:T(2,128)(2,1)S(1)} collective-permute-done((bf16[2,256,4,4,1]{1,4,3,2,0:T(2,128)(2,1)S(1)}, bf16[2,256,4,4,1]{1,4,3,2,0:T(2,128)(2,1)S(1)}, u32[]{:S(2)}, u32[]{:S(2)}) %collective-permute-start.17) | collective-permute-done | bytes 16416 | tf_op jit(solution)/shard_map/ppermute | solution.py:17
  147.5 2.8 %fusion.33 = f32[2,256,2,2,4]{1,0,4,3,2:T(2,128)S(1)} fusion(bf16[256,3,3,3,256]{0,4,3,2,1:T(8,128)(2,1)} %all-gather.3.cloned.1.call-done, bf16[2,256,4,4,6]{1,4,3,2,0:T(8,128)(2,1)S(1)} %pad_maximum_fusion.8), kind=kOutput, calls=%fused_computation.59 | convolution fusion | flops 113246208 | bytes 3670016 | tf_op jit(solution)/shard_map/conv_general_dilated | solution.py:31
  150.3 28.0 %all-gather.5.cloned.1.call-done = bf16[256,3,3,3,256]{0,4,3,2,1:T(8,128)(2,1)} async-done(((bf16[256,3,3,3,8]{0,4,3,2,1:T(8,128)(2,1)}), bf16[256,3,3,3,256]{0,4,3,2,1:T(8,128)(2,1)}) %all-gather.5.cloned.1.call-update) | async-done | bytes 3538960 | tf_op jit(solution)/shard_map/all_gather | solution.py:84
  178.3 2.9 %fusion.39 = (bf16[256,2,2,4]{0,3,2,1:T(4,128)(2,1)S(1)}, bf16[256,2,2,4]{0,3,2,1:T(4,128)(2,1)S(1)}) fusion(f32[2,256,2,2,4]{1,0,4,3,2:T(2,128)S(1)} %fusion.33, bf16[256,3,3,3,256]{0,4,3,2,1:T(8,128)(2,1)} %all-gather.5.cloned.1.call-done, bf16[1,256,4,4,6]{1,4,3,2,0:T(8,128)(2,1)S(1)} %slice.162), kind=kOutput, calls=%fused_computation.77 | convolution fusion | flops 56635392 | bytes 3637248 | tf_op jit(solution)/shard_map/conv_general_dilated | solution.py:31
  181.9 8.4 %all_to_all.27 = bf16[4,2,1024]{2,1,0:T(2,128)(2,1)S(1)} all-to-all(bf16[4,2,1024]{2,1,0:T(2,128)(2,1)S(1)} %reshape.75), channel_id=1, replica_groups=mesh['sx'=4,'sy'=8,'sz'=16] {'sx'}, dimensions={0} | all-to-all | bytes 32768 | tf_op jit(solution)/shard_map/all_to_all | solution.py:96
  191.1 8.4 %all_to_all.28 = bf16[8,2,512]{2,1,0:T(2,128)(2,1)S(1)} all-to-all(bf16[8,2,512]{2,1,0:T(2,128)(2,1)S(1)} %reshape.77), channel_id=1, replica_groups=mesh['sx'=4,'sy'=8,'sz'=16] {'sy'}, dimensions={0} | all-to-all | bytes 32768 | tf_op jit(solution)/shard_map/all_to_all | solution.py:95
  200.9 0.8 copy.82
  202.1 0.8 copy.83
  (88 shorter events, 11.0 us)
Async XLA Ops:
  7.2 103.1 %copy-start = (bf16[256,4,4,4,32]{0,4,3,2,1:T(8,128)(2,1)S(1)}, bf16[256,4,4,4,32]{0,4,3,2,1:T(8,128)(2,1)}, u32[]{:S(2)}) copy-start(bf16[256,4,4,4,32]{0,4,3,2,1:T(8,128)(2,1)} %param.20) | copy-start | bytes 3145732
  7.2 45.4 %copy-start.11 = (pred[8,3]{0,1:T(4,128)(4,1)S(1)}, pred[8,3]{0,1:T(4,128)(4,1)}, u32[]{:S(2)}) copy-start(pred[8,3]{0,1:T(4,128)(4,1)} %constant.19) | copy-start | bytes 76
  7.2 45.4 %copy-start.9 = (bf16[32,3,3,3,4]{0,4,3,2,1:T(4,128)(2,1)S(1)}, bf16[32,3,3,3,4]{0,4,3,2,1:T(4,128)(2,1)}, u32[]{:S(2)}) copy-start(bf16[32,3,3,3,4]{0,4,3,2,1:T(4,128)(2,1)} %param.14) | copy-start | bytes 20740
  7.2 45.4 %copy-start.8 = (bf16[32,3,3,3,4]{0,4,3,2,1:T(4,128)(2,1)S(1)}, bf16[32,3,3,3,4]{0,4,3,2,1:T(4,128)(2,1)}, u32[]{:S(2)}) copy-start(bf16[32,3,3,3,4]{0,4,3,2,1:T(4,128)(2,1)} %param.16) | copy-start | bytes 20740
  7.2 140.3 %all-gather.3.cloned.1.call-start = ((), (), s32[]{:S(2)}) async-start(), calls=%async_computation.2 | async-start | bytes 3649536 | tf_op jit(solution)/shard_map/all_gather | solution.py:83
  7.9 170.4 %all-gather.5.cloned.1.call-start = ((), (), s32[]{:S(2)}) async-start(), calls=%async_computation.3 | async-start | bytes 3649536 | tf_op jit(solution)/shard_map/all_gather | solution.py:84
  8.7 4.8 %collective-permute-start = (bf16[4,1,8,16]{3,2,1,0:T(8,128)(2,1)S(1)}, bf16[4,1,8,16]{3,2,1,0:T(8,128)(2,1)S(1)}, u32[]{:S(2)}, u32[]{:S(2)}) collective-permute-start(bf16[4,1,8,16]{3,2,1,0:T(8,128)(2,1)S(1)} %get-tuple-element.29), channel_id=1, source_target_pairs={{0,128},{128,256},{256,384},{1,129},{129,257},{257,385},{2,130},{1... | collective-permute-start | bytes 3080 | tf_op jit(solution)/shard_map/ppermute | solution.py:15
  12.2 5.5 %collective-permute-start.1 = (bf16[4,1,8,16]{3,2,1,0:T(8,128)(2,1)S(1)}, bf16[4,1,8,16]{3,2,1,0:T(8,128)(2,1)S(1)}, u32[]{:S(2)}, u32[]{:S(2)}) collective-permute-start(bf16[4,1,8,16]{3,2,1,0:T(8,128)(2,1)S(1)} %get-tuple-element.28), channel_id=1, source_target_pairs={{128,0},{256,128},{384,256},{129,1},{257,129},{385,257},{130,2},{2... | collective-permute-start | bytes 3080 | tf_op jit(solution)/shard_map/ppermute | solution.py:17
  17.8 2.6 %collective-permute-start.2 = (bf16[4,10,1,16]{3,2,1,0:T(2,128)(2,1)S(1)}, bf16[4,10,1,16]{3,2,1,0:T(2,128)(2,1)S(1)}, u32[]{:S(2)}, u32[]{:S(2)}) collective-permute-start(bf16[4,10,1,16]{3,2,1,0:T(2,128)(2,1)S(1)} %get-tuple-element.24), channel_id=1, source_target_pairs={{0,16},{16,32},{32,48},{48,64},{64,80},{80,96},{96,112},{1,17},{17... | collective-permute-start | bytes 3848 | tf_op jit(solution)/shard_map/ppermute | solution.py:15
  19.1 5.2 %collective-permute-start.3 = (bf16[4,10,1,16]{3,2,1,0:T(2,128)(2,1)S(1)}, bf16[4,10,1,16]{3,2,1,0:T(2,128)(2,1)S(1)}, u32[]{:S(2)}, u32[]{:S(2)}) collective-permute-start(bf16[4,10,1,16]{3,2,1,0:T(2,128)(2,1)S(1)} %get-tuple-element.25), channel_id=1, source_target_pairs={{16,0},{32,16},{48,32},{64,48},{80,64},{96,80},{112,96},{17,1},{33... | collective-permute-start | bytes 3848 | tf_op jit(solution)/shard_map/ppermute | solution.py:17
  24.5 22.6 %collective-permute-start.4 = (bf16[4,10,10,1]{3,2,1,0:T(8,128)(2,1)S(1)}, bf16[4,10,10,1]{3,2,1,0:T(8,128)(2,1)S(1)}, u32[]{:S(2)}, u32[]{:S(2)}) collective-permute-start(bf16[4,10,10,1]{3,2,1,0:T(8,128)(2,1)S(1)} %get-tuple-element.22), channel_id=1, source_target_pairs={{0,1},{1,2},{2,3},{3,4},{4,5},{5,6},{6,7},{7,8},{8,9},{9,10},{10,1... | collective-permute-start | bytes 2408 | tf_op jit(solution)/shard_map/ppermute | solution.py:15
  33.6 17.1 %collective-permute-start.5 = (bf16[4,10,10,1]{3,2,1,0:T(8,128)(2,1)S(1)}, bf16[4,10,10,1]{3,2,1,0:T(8,128)(2,1)S(1)}, u32[]{:S(2)}, u32[]{:S(2)}) collective-permute-start(bf16[4,10,10,1]{3,2,1,0:T(8,128)(2,1)S(1)} %get-tuple-element.23), channel_id=1, source_target_pairs={{1,0},{2,1},{3,2},{4,3},{5,4},{6,5},{7,6},{8,7},{9,8},{10,9},{11,1... | collective-permute-start | bytes 2408 | tf_op jit(solution)/shard_map/ppermute | solution.py:17
  52.6 1.8 copy-start.2
  55.0 8.6 %collective-permute-start.6 = (bf16[2,32,1,8,16]{1,3,4,2,0:T(8,128)(2,1)S(1)}, bf16[2,32,1,8,16]{1,3,4,2,0:T(8,128)(2,1)S(1)}, u32[]{:S(2)}, u32[]{:S(2)}) collective-permute-start(bf16[2,32,1,8,16]{1,3,4,2,0:T(8,128)(2,1)S(1)} %get-tuple-element.18), channel_id=1, source_target_pairs={{0,128},{128,256},{256,384},{1,129},{129,257},{257,385},{2,130},{1... | collective-permute-start | bytes 49160 | tf_op jit(solution)/shard_map/ppermute | solution.py:15
  61.7 6.7 %collective-permute-start.7 = (bf16[2,32,1,8,16]{1,3,4,2,0:T(8,128)(2,1)S(1)}, bf16[2,32,1,8,16]{1,3,4,2,0:T(8,128)(2,1)S(1)}, u32[]{:S(2)}, u32[]{:S(2)}) collective-permute-start(bf16[2,32,1,8,16]{1,3,4,2,0:T(8,128)(2,1)S(1)} %get-tuple-element.19), channel_id=1, source_target_pairs={{128,0},{256,128},{384,256},{129,1},{257,129},{385,257},{130,2},{2... | collective-permute-start | bytes 49160 | tf_op jit(solution)/shard_map/ppermute | solution.py:17
  68.6 5.0 %collective-permute-start.8 = (bf16[2,32,10,1,16]{1,3,4,2,0:T(2,128)(2,1)S(1)}, bf16[2,32,10,1,16]{1,3,4,2,0:T(2,128)(2,1)S(1)}, u32[]{:S(2)}, u32[]{:S(2)}) collective-permute-start(bf16[2,32,10,1,16]{1,3,4,2,0:T(2,128)(2,1)S(1)} %get-tuple-element.16), channel_id=1, source_target_pairs={{0,16},{16,32},{32,48},{48,64},{64,80},{80,96},{96,112},{1,17},{17... | collective-permute-start | bytes 61448 | tf_op jit(solution)/shard_map/ppermute | solution.py:15
  72.3 6.1 %collective-permute-start.9 = (bf16[2,32,10,1,16]{1,3,4,2,0:T(2,128)(2,1)S(1)}, bf16[2,32,10,1,16]{1,3,4,2,0:T(2,128)(2,1)S(1)}, u32[]{:S(2)}, u32[]{:S(2)}) collective-permute-start(bf16[2,32,10,1,16]{1,3,4,2,0:T(2,128)(2,1)S(1)} %get-tuple-element.17), channel_id=1, source_target_pairs={{16,0},{32,16},{48,32},{64,48},{80,64},{96,80},{112,96},{17,1},{33... | collective-permute-start | bytes 61448 | tf_op jit(solution)/shard_map/ppermute | solution.py:17
  78.6 11.4 %collective-permute-start.10 = (bf16[2,32,10,10,1]{1,3,4,2,0:T(8,128)(2,1)S(1)}, bf16[2,32,10,10,1]{1,3,4,2,0:T(8,128)(2,1)S(1)}, u32[]{:S(2)}, u32[]{:S(2)}) collective-permute-start(bf16[2,32,10,10,1]{1,3,4,2,0:T(8,128)(2,1)S(1)} %get-tuple-element.12), channel_id=1, source_target_pairs={{0,1},{1,2},{2,3},{3,4},{4,5},{5,6},{6,7},{7,8},{8,9},{9,10},{10,1... | collective-permute-start | bytes 38408 | tf_op jit(solution)/shard_map/ppermute | solution.py:15
  85.3 10.4 %collective-permute-start.11 = (bf16[2,32,10,10,1]{1,3,4,2,0:T(8,128)(2,1)S(1)}, bf16[2,32,10,10,1]{1,3,4,2,0:T(8,128)(2,1)S(1)}, u32[]{:S(2)}, u32[]{:S(2)}) collective-permute-start(bf16[2,32,10,10,1]{1,3,4,2,0:T(8,128)(2,1)S(1)} %get-tuple-element.13), channel_id=1, source_target_pairs={{1,0},{2,1},{3,2},{4,3},{5,4},{6,5},{7,6},{8,7},{9,8},{10,9},{11,1... | collective-permute-start | bytes 38408 | tf_op jit(solution)/shard_map/ppermute | solution.py:17
  97.3 0.9 copy-start.6
  103.9 2.5 %copy-start.7 = (bf16[32,3,3,3,32]{4,0,3,2,1:T(8,128)(2,1)S(1)}, bf16[32,3,3,3,32]{4,0,3,2,1:T(8,128)(2,1)}, u32[]{:S(2)}) copy-start(bf16[32,3,3,3,32]{4,0,3,2,1:T(8,128)(2,1)} %param.17) | copy-start | bytes 165892
  103.9 2.5 %copy-start.10 = (pred[16,3]{0,1:T(4,128)(4,1)S(1)}, pred[16,3]{0,1:T(4,128)(4,1)}, u32[]{:S(2)}) copy-start(pred[16,3]{0,1:T(4,128)(4,1)} %constant.18) | copy-start | bytes 148
  109.1 0.7 copy-start.3
  110.1 1.3 copy-start.5
  110.2 2.1 copy-start.1
  112.4 6.9 %collective-permute-start.12 = (bf16[2,256,1,2,4]{1,4,3,2,0:T(4,128)(2,1)S(1)}, bf16[2,256,1,2,4]{1,4,3,2,0:T(4,128)(2,1)S(1)}, u32[]{:S(2)}, u32[]{:S(2)}) collective-permute-start(bf16[2,256,1,2,4]{1,4,3,2,0:T(4,128)(2,1)S(1)} %get-tuple-element.36), channel_id=1, source_target_pairs={{0,128},{128,256},{256,384},{1,129},{129,257},{257,385},{2,130},{1... | collective-permute-start | bytes 24584 | tf_op jit(solution)/shard_map/ppermute | solution.py:15
  117.9 5.5 %collective-permute-start.13 = (bf16[2,256,1,2,4]{1,4,3,2,0:T(4,128)(2,1)S(1)}, bf16[2,256,1,2,4]{1,4,3,2,0:T(4,128)(2,1)S(1)}, u32[]{:S(2)}, u32[]{:S(2)}) collective-permute-start(bf16[2,256,1,2,4]{1,4,3,2,0:T(4,128)(2,1)S(1)} %get-tuple-element.37), channel_id=1, source_target_pairs={{128,0},{256,128},{384,256},{129,1},{257,129},{385,257},{130,2},{2... | collective-permute-start | bytes 24584 | tf_op jit(solution)/shard_map/ppermute | solution.py:17
  123.5 6.1 %collective-permute-start.14 = (bf16[2,256,4,1,4]{1,4,3,2,0:T(4,128)(2,1)S(1)}, bf16[2,256,4,1,4]{1,4,3,2,0:T(4,128)(2,1)S(1)}, u32[]{:S(2)}, u32[]{:S(2)}) collective-permute-start(bf16[2,256,4,1,4]{1,4,3,2,0:T(4,128)(2,1)S(1)} %get-tuple-element.30), channel_id=1, source_target_pairs={{0,16},{16,32},{32,48},{48,64},{64,80},{80,96},{96,112},{1,17},{17... | collective-permute-start | bytes 49160 | tf_op jit(solution)/shard_map/ppermute | solution.py:15
  128.3 4.1 %collective-permute-start.15 = (bf16[2,256,4,1,4]{1,4,3,2,0:T(4,128)(2,1)S(1)}, bf16[2,256,4,1,4]{1,4,3,2,0:T(4,128)(2,1)S(1)}, u32[]{:S(2)}, u32[]{:S(2)}) collective-permute-start(bf16[2,256,4,1,4]{1,4,3,2,0:T(4,128)(2,1)S(1)} %get-tuple-element.31), channel_id=1, source_target_pairs={{16,0},{32,16},{48,32},{64,48},{80,64},{96,80},{112,96},{17,1},{33... | collective-permute-start | bytes 49160 | tf_op jit(solution)/shard_map/ppermute | solution.py:17
  132.5 10.7 %collective-permute-start.16 = (bf16[2,256,4,4,1]{1,4,3,2,0:T(2,128)(2,1)S(1)}, bf16[2,256,4,4,1]{1,4,3,2,0:T(2,128)(2,1)S(1)}, u32[]{:S(2)}, u32[]{:S(2)}) collective-permute-start(bf16[2,256,4,4,1]{1,4,3,2,0:T(2,128)(2,1)S(1)} %get-tuple-element.26), channel_id=1, source_target_pairs={{0,1},{1,2},{2,3},{3,4},{4,5},{5,6},{6,7},{7,8},{8,9},{9,10},{10,1... | collective-permute-start | bytes 49160 | tf_op jit(solution)/shard_map/ppermute | solution.py:15
  137.5 9.8 %collective-permute-start.17 = (bf16[2,256,4,4,1]{1,4,3,2,0:T(2,128)(2,1)S(1)}, bf16[2,256,4,4,1]{1,4,3,2,0:T(2,128)(2,1)S(1)}, u32[]{:S(2)}, u32[]{:S(2)}) collective-permute-start(bf16[2,256,4,4,1]{1,4,3,2,0:T(2,128)(2,1)S(1)} %get-tuple-element.27), channel_id=1, source_target_pairs={{1,0},{2,1},{3,2},{4,3},{5,4},{6,5},{7,6},{8,7},{9,8},{10,9},{11,1... | collective-permute-start | bytes 49160 | tf_op jit(solution)/shard_map/ppermute | solution.py:17
  181.6 19.2 %copy-start.4 = (f32[8]{0:T(128)S(1)}, f32[8]{0:T(128)}, u32[]{:S(2)}) copy-start(f32[8]{0:T(128)} %param.24) | copy-start | bytes 100
Sparse Core Ops, SparseCore 0:
  10.1 90.2 all-gather.2
  102.5 75.7 all-gather.4
where the time goes:
time: 211 us; the launch traced here: 210 us
  waiting for transfers between devices  76 us (36%)
  starting transfers between devices  68.8 us (33%)
  blocking collectives  16.9 us (8%)
  between operations  14.8 us (7%)
  matrix products  13.1 us (6%)
  local copies, waits for them, and re-layouts  13 us (6%)
  other arithmetic  7.3 us (3%)
    ppermute x9, starting transfers between devices, with_halo(): lax.ppermute(tail, axis, [(i, (i + 1) % count) for i in range(ends)])  46.3 us
    ppermute x9, waiting for transfers between devices, with_halo(): lax.ppermute(head, axis, [((i + 1) % count, i) for i in range(ends)])  37.3 us
    all_gather x1, waiting for transfers between devices, body(): lax.all_gather(conv3_probe, ('sx', 'sy'), axis=4, tiled=True)  28 us
    ppermute x9, starting transfers between devices, with_halo(): lax.ppermute(head, axis, [((i + 1) % count, i) for i in range(ends)])  22.4 us
    conv_general_dilated x7, matrix products, cells(): lax.conv_general_dilated(volume, weight, (stride, stride, stride), 'VALID...  13.1 us
    ppermute x9, waiting for transfers between devices, with_halo(): lax.ppermute(tail, axis, [(i, (i + 1) % count) for i in range(ends)])  9.9 us
    all_to_all x1, blocking collectives, body(): lax.all_to_all(totals.astype(jnp.bfloat16), 'sx', split_axis=1, concat_ax...  8.44 us
    all_to_all x1, blocking collectives, body(): lax.all_to_all(lax.all_to_all(totals.astype(jnp.bfloat16), 'sx', split_ax...  8.42 us
  transfers between devices with their start and end apart: 20, of which 14 were waited for; matrix products, arithmetic and copies ran while one was open for 12% of the time, Pallas kernels for 0%

commit v1 on v0

v1 whole, which is shorter than its diff:
```python
import jax
import jax.numpy as jnp
from jax import lax
from jax.experimental import pallas as pl
from jax.experimental.pallas import tpu as pltpu
from jax.sharding import PartitionSpec as P

BF = jnp.bfloat16
F32 = jnp.float32
VM = pl.BlockSpec(memory_space=pltpu.VMEM)
SM = pl.BlockSpec(memory_space=pltpu.SMEM)


def call(kernel, outs, scratch=(), specs=None, flops=1000000):
    return pl.pallas_call(
        kernel,
        out_shape=outs,
        in_specs=specs,
        out_specs=jax.tree.map(lambda _: VM, outs),
        scratch_shapes=list(scratch),
        cost_estimate=pl.CostEstimate(flops=flops, bytes_accessed=100000, transcendentals=0),
    )


def silu_pair(v, direction):
    s = 1.0 / (1.0 + jnp.exp(-v))
    return v * s, s * (1.0 + v * (1.0 - s)) * direction


def iota(shape, dim):
    return lax.broadcasted_iota(jnp.int32, shape, dim)


def pack_kernel(dens, own, to_right, to_left):
    total = jnp.zeros((64, 64), F32)
    for c in range(4):
        rows = dens[c].astype(F32).reshape(64, 16).astype(BF)
        place = (iota((16, 64), 1) == 4 * iota((16, 64), 0) + c).astype(BF)
        total += jnp.dot(rows, place, preferred_element_type=F32)
    own[...] = total.astype(BF)
    for ref, at in ((to_right, 32), (to_left, 0)):
        ref[...] = jnp.concatenate(
            [total[16 * g : 16 * g + 16, at : at + 32] for g in range(4)], axis=1
        ).astype(BF)


SIDES = [(dx, dy) for dx in (-1, 0, 1) for dy in (-1, 0, 1) if dx or dy]


def inside(dx, dy):
    sx, sy = lax.axis_index("sx") + dx, lax.axis_index("sy") + dy
    ok = (sx >= 0) & (sx < 4) & (sy >= 0) & (sy < 8)
    return ok, jnp.where(ok, sx * 8 + sy, 0)


def face_kernel(own, left, right, block, slots, wide):
    def unpack(ref):
        v = ref[...].astype(F32)
        return jnp.concatenate([v[:, 32 * g : 32 * g + 32] for g in range(4)], axis=0)

    cells = jnp.concatenate([unpack(left), own[...].astype(F32), unpack(right)], axis=1)
    block[...] = cells.astype(BF)
    wide[...] = jnp.zeros_like(wide)
    for dx, dy in SIDES:
        ok, at = inside(dx, dy)

        @pl.when(ok)
        def _(dx=dx, dy=dy, at=at):
            xs = range(8) if dx == 0 else ((6, 7) if dx > 0 else (0, 1))
            for j, x in enumerate(xs):
                if dy == 0:
                    wide[at, 8 * j : 8 * j + 8, :] = cells[8 * x : 8 * x + 8]
                else:
                    y = 6 if dy > 0 else 0
                    wide[at, 2 * j : 2 * j + 2, :] = cells[8 * x + y : 8 * x + y + 2]

    slots[...] = wide[...].astype(BF)


def lift_kernel(
    block, slots, t1, b1, t2, b2, lift_w, lift_p, b3, out, dens, win, acc1, hp, acc2, lhs, got
):
    dens[...] = jnp.zeros_like(dens)
    got[...] = slots[...].astype(F32)
    cells = block[...].astype(F32)
    for x in range(8):
        dens[2 + x, 2:10, :] = cells[8 * x : 8 * x + 8]
    for dx, dy in SIDES:
        ok, at = inside(dx, dy)

        @pl.when(ok)
        def _(dx=dx, dy=dy, at=at):
            xs = range(2, 10) if dx == 0 else ((10, 11) if dx > 0 else (0, 1))
            for j, x in enumerate(xs):
                if dy == 0:
                    dens[x, 2:10, :] = got[at, 8 * j : 8 * j + 8, :]
                else:
                    y = 10 if dy > 0 else 0
                    dens[x, y : y + 2, :] = got[at, 2 * j : 2 * j + 2, :]

    lane = iota((8, 128), 1)

    def windows(x, carry):
        shifted = []
        for y in range(12):
            row = jnp.broadcast_to(dens[x, y : y + 1, :], (8, 128))
            first = pltpu.roll(row, 8, 1, stride=16, stride_axis=0)
            shifted.append((first, pltpu.roll(first, 32, 1), pltpu.roll(first, 64, 1)))
        for y in range(10):
            win[x, 8 * y : 8 * y + 8, :] = jnp.where(
                lane < 32, shifted[y][0], jnp.where(lane < 64, shifted[y + 1][1], shifted[y + 2][2])
            )
        return carry

    lax.fori_loop(0, 12, windows, 0)

    rows = jnp.concatenate(
        [win[p : p + 10].reshape(800, 128).astype(BF) for p in range(3)], axis=1
    )
    acc1[...] = jnp.dot(rows, t1[...], preferred_element_type=F32)

    fine = 16 * lax.axis_index("sz") + 4 * (6 - iota((8, 256), 0)) - 1 + iota((8, 256), 1) // 32
    zmask = jnp.where((fine >= 0) & (fine < 256), 1.0, 0.0)
    bias1 = jnp.concatenate([b1[...]] * 6 + [jnp.zeros((1, 64), F32)], axis=1)

    def first(x, carry):
        gx = 8 * lax.axis_index("sx") + x - 1
        okx = (gx >= 0) & (gx < 32)
        for y in range(10):
            gy = 8 * lax.axis_index("sy") + y - 1
            ok = okx & (gy >= 0) & (gy < 64)
            mask = jnp.where(ok, zmask, 0.0)
            at = pl.ds(pl.multiple_of(80 * x + 8 * y, 8), 8)
            h, d = silu_pair(acc1[at, 0:256] + bias1, acc1[at, 256:512])
            hp[x, y] = jnp.concatenate([h * mask, d * mask], axis=0).astype(BF)
        return carry

    lax.fori_loop(0, 10, first, 0)

    for t in range(9):
        p, q = divmod(t, 3)
        part = lax.dot_general(
            hp[p : p + 8, q : q + 8].reshape(1024, 256),
            t2[t],
            (((1,), (1,)), ((), ())),
            preferred_element_type=F32,
        )
        if t == 0:
            acc2[...] = part
        else:
            acc2[...] += part

    bias2 = jnp.concatenate([b2[...]] * 4, axis=1)
    for x in range(8):
        for y in range(8):
            r = 16 * (8 * x + y)
            h, d = silu_pair(
                acc2[r : r + 8, 0:128] + bias2,
                acc2[r : r + 8, 128:256] + acc2[r + 8 : r + 16, 0:128],
            )
            at = 16 * (2 * (x // 4) + y // 4)
            tap = 128 * (4 * (x % 4) + y % 4)
            lhs[at : at + 16, tap : tap + 128] = jnp.concatenate([h, d], axis=0).astype(BF)

    left = lhs[...]
    by_w = jnp.dot(left, lift_w[...], preferred_element_type=F32)
    by_p = jnp.dot(left, lift_p[...], preferred_element_type=F32)
    level = 7 - iota((8, 256), 0)
    coarse = 4 * lax.axis_index("sz") + level - 1
    mask = jnp.where((level < 6) & (coarse >= 0) & (coarse < 64), 1.0, 0.0)
    hs, ds = [], []
    for k in range(4):
        h, d = silu_pair(
            by_w[16 * k : 16 * k + 8] + b3[...],
            by_p[16 * k : 16 * k + 8] + by_w[16 * k + 8 : 16 * k + 16],
        )
        hs.append(h * mask)
        ds.append(d * mask)
    turned = jnp.concatenate(hs + ds, axis=0).T
    for m in range(16):
        chunk = jnp.concatenate(
            [turned[16 * m : 16 * m + 8], turned[16 * m + 8 : 16 * m + 16]], axis=1
        ).astype(BF)
        out[2 * m] = chunk
        out[2 * m + 1] = chunk


def last_kernel(got, w_own, p_own, w_far, p_far, out, flat, turned):
    flat[...] = got[...].astype(F32).reshape(256, 128)
    for c in range(8):
        turned[pl.ds(c, 128, stride=8), 0:32] = flat[pl.ds(c, 32, stride=8), :].T
    lane = iota((8, 128), 1)
    cx, cy, bx, by = lane >> 6, (lane >> 5) & 1, (lane >> 3) & 3, lane & 7

    def shift_x(v, by_one):
        if by_one == 0:
            return v
        if by_one > 0:
            s = jnp.where(cx == 0, pltpu.roll(v, 64, 1), pltpu.roll(v, 56, 1))
            return jnp.where((cx == 1) & (bx == 3), 0.0, s)
        s = jnp.where(cx == 1, pltpu.roll(v, 64, 1), pltpu.roll(v, 72, 1))
        return jnp.where((cx == 0) & (bx == 0), 0.0, s)

    def shift_y(v, by_one):
        if by_one == 0:
            return v
        if by_one > 0:
            s = jnp.where(cy == 0, pltpu.roll(v, 96, 1), pltpu.roll(v, 31, 1))
            return jnp.where((cy == 1) & (by == 7), 0.0, s)
        s = jnp.where(cy == 1, pltpu.roll(v, 32, 1), pltpu.roll(v, 97, 1))
        return jnp.where((cy == 0) & (by == 0), 0.0, s)

    def columns(k, kind):
        pieces = {}
        for z in range(6):
            tile = jnp.concatenate(
                [
                    turned[pl.ds(8 * (64 * k + 32 * kind + 8 * xy + 7 - z), 8), 0:32]
                    for xy in range(4)
                ],
                axis=1,
            )
            for p in range(3):
                moved = shift_x(tile, p - 1)
                for q in range(3):
                    pieces[p, q, z] = shift_y(moved, q - 1)
        return jnp.concatenate(
            [
                jnp.concatenate([pieces[p, q, r + z] for z in range(4)], axis=1)
                for p in range(3)
                for q in range(3)
                for r in range(3)
            ],
            axis=0,
        ).astype(BF)

    core = lax.axis_index("sy") % 2
    first = core == 0

    def pick(a, b):
        return jnp.where(first, a[...], b[...])

    def product(w, x):
        return lax.dot_general(w, x, (((0,), (0,)), ((), ())), preferred_element_type=F32)

    pre, dot = 0.0, 0.0
    for k in range(2):
        w = pick(w_own, w_far) if k == 0 else pick(w_far, w_own)
        d = pick(p_own, p_far) if k == 0 else pick(p_far, p_own)
        h_cols = columns(k, 0)
        pre = pre + product(w, h_cols)
        dot = dot + product(d, h_cols) + product(w, columns(k, 1))
    pre = pre.reshape(16, 2, 8, 512)
    dot = dot.reshape(16, 2, 8, 512)
    pre = jnp.where(first, pre[:, 0], pre[:, 1])
    dot = jnp.where(first, dot[:, 0], dot[:, 1])
    out[...] = jnp.concatenate([pre, dot], axis=1).astype(BF)


def sum_kernel(got, bias, features, tangent, rows):
    total = got[0].astype(F32)
    for s in range(1, 16):
        total = total + got[s].astype(F32)
    level = iota((16, 512), 0)
    for o in range(8):
        total = total + jnp.where(level == o, bias[o], 0.0)
    total = total.astype(BF)
    here, there = iota((128, 128), 0), iota((128, 128), 1)
    gx = 2 * ((here >> 3) & 3) + (here >> 6)
    gy = 2 * (here & 7) + ((here >> 5) & 1)
    place = (there == 16 * gx + gy).astype(BF)
    for z in range(4):
        rows[pl.ds(z, 16, stride=4), :] = jnp.dot(
            total[:, 128 * z : 128 * z + 128], place, preferred_element_type=F32
        )
    for x in range(8):
        moved = rows[...] if x == 0 else pltpu.roll(rows[...], 128 - 16 * x, 1)
        for o in range(8):
            features[o, x] = moved[4 * o : 4 * o + 4, 0:16].astype(BF)
            tangent[o, x] = moved[32 + 4 * o : 32 + 4 * o + 4, 0:16].astype(BF)


def first_matrix(w, p):
    def bands(v):
        v = jnp.transpose(v, (1, 2, 3, 4, 0)).reshape(3, 3, 12, 32)
        wide = [jnp.pad(v, ((0, 0), (0, 0), (4 * z, 20 - 4 * z), (0, 0))) for z in range(6)]
        return jnp.concatenate(wide + [jnp.zeros((3, 3, 32, 64), BF)], axis=3)

    both = jnp.concatenate([bands(w), bands(p)], axis=3).reshape(3, 96, 512)
    return jnp.pad(both, ((0, 0), (0, 32), (0, 0))).reshape(384, 512)


def second_matrix(w, p):
    def bands(v):
        v = jnp.transpose(v, (1, 2, 0, 3, 4)).reshape(9, 32, 96)
        wide = [jnp.pad(v, ((0, 0), (0, 0), (32 * z, 160 - 32 * z))) for z in range(4)]
        return jnp.concatenate(wide, axis=1)

    return jnp.concatenate([bands(w), bands(p)], axis=1)


def body(
    density,
    conv1_weight,
    conv1_bias,
    conv1_probe,
    conv2_weight,
    conv2_bias,
    conv2_probe,
    lift_weight,
    lift_bias,
    lift_probe,
    conv3_weight,
    conv3_bias,
    conv3_probe,
):
    S = jax.ShapeDtypeStruct
    own, to_right, to_left = call(
        pack_kernel, (S((64, 64), BF), S((16, 128), BF), S((16, 128), BF)), specs=[VM]
    )(density)
    from_left = lax.ppermute(to_right, "sz", [(i, i + 1) for i in range(15)])
    from_right = lax.ppermute(to_left, "sz", [(i + 1, i) for i in range(15)])

    def flat3(v):
        return jnp.transpose(v, (1, 2, 3, 4, 0)).reshape(216, 256)

    w3, p3 = flat3(conv3_weight), flat3(conv3_probe)
    swap = [(i, i ^ 1) for i in range(8)]
    w3_far, p3_far = lax.ppermute(w3, "sy", swap), lax.ppermute(p3, "sy", swap)
    t1 = first_matrix(conv1_weight, conv1_probe)
    t2 = second_matrix(conv2_weight, conv2_probe)

    block, slots = call(
        face_kernel,
        (S((64, 128), BF), S((32, 16, 128), BF)),
        scratch=[pltpu.VMEM((32, 16, 128), F32)],
        specs=[VM] * 3,
    )(own, from_left, from_right)
    near = lax.all_to_all(slots, ("sx", "sy"), 0, 0, tiled=True)

    def flat_lift(v):
        return jnp.transpose(v, (1, 2, 3, 4, 0)).reshape(2048, 256)

    lifted = call(
        lift_kernel,
        S((32, 8, 128), BF),
        scratch=[
            pltpu.VMEM((12, 16, 128), F32),
            pltpu.VMEM((12, 80, 128), F32),
            pltpu.VMEM((800, 512), F32),
            pltpu.VMEM((10, 10, 16, 256), BF),
            pltpu.VMEM((1024, 256), F32),
            pltpu.VMEM((64, 2048), BF),
            pltpu.VMEM((32, 16, 128), F32),
        ],
        specs=[VM] * 9,
        flops=10000000,
    )(
        block,
        near,
        t1,
        conv1_bias.reshape(1, 32),
        t2,
        conv2_bias.reshape(1, 32),
        flat_lift(lift_weight),
        flat_lift(lift_probe),
        lift_bias.reshape(1, 256),
    )
    gathered = lax.all_to_all(lifted, ("sx", "sy"), 0, 0, tiled=True)
    parts = call(
        last_kernel,
        S((16, 16, 512), BF),
        scratch=[pltpu.VMEM((256, 128), F32), pltpu.VMEM((1024, 128), F32)],
        specs=[VM] * 5,
        flops=10000000,
    )(gathered, w3, p3, w3_far, p3_far)
    same_core = [[8 * x + 2 * z + c for x in range(4) for z in range(4)] for c in range(2)]
    mine = lax.all_to_all(
        parts, ("sx", "sy"), 0, 0, axis_index_groups=same_core, tiled=True
    )
    features, tangent = call(
        sum_kernel,
        (S((8, 8, 4, 16), BF), S((8, 8, 4, 16), BF)),
        scratch=[pltpu.VMEM((64, 128), F32)],
        specs=[VM, SM],
    )(mine, conv3_bias)
    return jnp.transpose(features, (0, 1, 3, 2)), jnp.transpose(tangent, (0, 1, 3, 2))


def solution(mesh):
    placed = (
        P(None, "sx", "sy", "sz"),
        P(),
        P(),
        P(),
        P(),
        P(),
        P(),
        P(),
        P(),
        P(),
        P(None, None, None, None, ("sx", "sy")),
        P(("sx", "sy")),
        P(None, None, None, None, ("sx", "sy")),
    )
    return jax.shard_map(
        body,
        mesh=mesh,
        in_specs=placed,
        out_specs=(P(("sx", "sy"), None, None, "sz"), P(("sx", "sy"), None, None, "sz")),
        check_vma=False,
    )
```

time: 211 us -> 84.8 us (0.40)
  waiting for transfers between devices: 76 us -> 13 us
  starting transfers between devices: 68.8 us -> 30.7 us
  Pallas kernels: 0 us -> 16.4 us
  between operations: 14.8 us -> 0.89 us
  matrix products: 13.1 us -> 0 us
  other arithmetic: 7.3 us -> 0 us
  local copies, waits for them, and re-layouts: 13 us -> 6.21 us
    ppermute x18 -> x4, starting transfers between devices: 68.7 us -> 19.2 us  [the longest x1 9.08 us: body(): from_left = lax.ppermute(to_right, 'sz', [(i, i + 1) for i in range(15)])]
    ppermute x18 -> x4, waiting for transfers between devices: 47.2 us -> 3.68 us  [the longest x1 2.74 us: body(): from_right = lax.ppermute(to_left, 'sz', [(i + 1, i) for i in range(15)])]
    all_gather x2 -> x0, waiting for transfers between devices: 28.1 us -> none  [the longest x1 28 us: body(): lax.all_gather(conv3_probe, ('sx', 'sy'), axis=4, tiled=True)]
    pallas_call x0 -> x5, Pallas kernels: none -> 16.4 us  [the longest x1 8.22 us: body(): call(lift_kernel, S((32, 8, 128), BF), scratch=[pltpu.VMEM((12, 16, 128),...]
    conv_general_dilated x7 -> x0, matrix products: 13.1 us -> none  [cells(): lax.conv_general_dilated(volume, weight, (stride, stride, stride), 'VALID...]
    all_to_all x0 -> x2, starting transfers between devices: none -> 11.5 us  [the longest x1 7.65 us: body(): near = lax.all_to_all(slots, ('sx', 'sy'), 0, 0, tiled=True)]
    all_to_all x0 -> x2, waiting for transfers between devices: none -> 9.37 us  [the longest x1 6.68 us: body(): near = lax.all_to_all(slots, ('sx', 'sy'), 0, 0, tiled=True)]
    unnamed x35 -> x29, local copies, waits for them, and re-layouts: 6.08 us -> 2.49 us
  transfers between devices with their start and end apart: 20 -> 6, of which waited for: 14 -> 4; matrix products, arithmetic and copies ran while one was open for 12% -> 5% of each run, Pallas kernels for 0% -> 0%
where the time goes in v1:
time: 84.8 us; the launch traced here: 84.1 us
  starting transfers between devices  30.7 us (36%)
  blocking collectives  16.8 us (20%)
  Pallas kernels  16.4 us (19%)
  waiting for transfers between devices  13 us (15%)
  local copies, waits for them, and re-layouts  6.21 us (7%)
  between operations  0.89 us (1%)
    all_to_all x1, blocking collectives, body(): lax.all_to_all(parts, ('sx', 'sy'), 0, 0, axis_index_groups=same_core, ti...  16.8 us
    ppermute x1, starting transfers between devices, body(): from_left = lax.ppermute(to_right, 'sz', [(i, i + 1) for i in range(15)])  9.08 us
    pallas_call x1, Pallas kernels, body(): call(lift_kernel, S((32, 8, 128), BF), scratch=[pltpu.VMEM((12, 16, 128),...  8.22 us
    all_to_all x1, starting transfers between devices, body(): near = lax.all_to_all(slots, ('sx', 'sy'), 0, 0, tiled=True)  7.65 us
    all_to_all x1, waiting for transfers between devices, body(): near = lax.all_to_all(slots, ('sx', 'sy'), 0, 0, tiled=True)  6.68 us
    ppermute x1, starting transfers between devices, body(): from_right = lax.ppermute(to_left, 'sz', [(i + 1, i) for i in range(15)])  5.82 us
    all_to_all x1, starting transfers between devices, body(): gathered = lax.all_to_all(lifted, ('sx', 'sy'), 0, 0, tiled=True)  3.86 us
    pallas_call x1, Pallas kernels, body(): call(last_kernel, S((16, 16, 512), BF), scratch=[pltpu.VMEM((256, 128), F...  3.03 us
  transfers between devices with their start and end apart: 6, of which 4 were waited for; matrix products, arithmetic and copies ran while one was open for 5% of the time, Pallas kernels for 0%

profile of v1, /device:TPU:6, one launch (start us, length us, event | category | flops | bytes accessed | tf_op | source)
XLA Modules:
  0.0 84.1 jit_solution(6781584903769242948)
XLA Ops:
  0.6 0.0 copy-start.3
  0.6 1.7 %shard_map.140 = (bf16[64,64]{1,0:T(8,128)(2,1)}, bf16[16,128]{1,0:T(8,128)(2,1)}, bf16[16,128]{1,0:T(8,128)(2,1)}) custom-call(bf16[4,8,8,16]{3,2,1,0:T(8,128)(2,1)} %dens.1), custom_call_target="tpu_custom_call" | custom-call | flops 1000000 | bytes 100000 | tf_op jit(solution)/shard_map/pallas_call | solution.py:318
  2.3 9.1 %collective-permute-start = (bf16[16,128]{1,0:T(8,128)(2,1)}, bf16[16,128]{1,0:T(8,128)(2,1)S(1)}, u32[]{:S(2)}, u32[]{:S(2)}) collective-permute-start(bf16[16,128]{1,0:T(8,128)(2,1)} %get-tuple-element.10), channel_id=1, source_target_pairs={{0,1},{1,2},{2,3},{3,4},{4,5},{5,6},{6,7},{7,8},{8,9},{9,10},{10,1... | collective-permute-start | bytes 12296 | tf_op jit(solution)/shard_map/ppermute | solution.py:321
  11.4 5.8 %collective-permute-start.1 = (bf16[16,128]{1,0:T(8,128)(2,1)}, bf16[16,128]{1,0:T(8,128)(2,1)S(1)}, u32[]{:S(2)}, u32[]{:S(2)}) collective-permute-start(bf16[16,128]{1,0:T(8,128)(2,1)} %get-tuple-element.11), channel_id=1, source_target_pairs={{1,0},{2,1},{3,2},{4,3},{5,4},{6,5},{7,6},{8,7},{9,8},{10,9},{11,1... | collective-permute-start | bytes 12296 | tf_op jit(solution)/shard_map/ppermute | solution.py:322
  17.3 0.8 reshape.44
  18.0 0.1 fusion
  18.1 0.8 reshape.43
  18.9 0.1 fusion.1
  19.0 0.0 copy-done.3
  19.0 0.2 copy.17
  19.1 0.2 reshape.48
  19.3 0.1 pad_dynamic-update-slice_fusion.6
  19.4 0.1 pad_dynamic-update-slice_fusion.5
  19.6 0.0 collective-permute-done.left
  19.6 0.0 copy-start.9
  19.6 2.7 %collective-permute-done.1.right = bf16[16,128]{1,0:T(8,128)(2,1)S(1)} collective-permute-done((bf16[16,128]{1,0:T(8,128)(2,1)}, bf16[16,128]{1,0:T(8,128)(2,1)S(1)}, u32[]{:S(2)}, u32[]{:S(2)}) %collective-permute-start.1) | collective-permute-done | bytes 4128 | tf_op jit(solution)/shard_map/ppermute | solution.py:322
  22.3 0.0 copy-done.9
  22.3 0.6 copy-done.10
  22.9 1.5 %shard_map.141 = (bf16[64,128]{1,0:T(8,128)(2,1)}, bf16[32,16,128]{2,1,0:T(8,128)(2,1)}) custom-call(bf16[64,64]{1,0:T(8,128)(2,1)} %get-tuple-element.9.own, bf16[16,128]{1,0:T(8,128)(2,1)} %copy-done.9, bf16[16,128]{1,0:T(8,128)(2,1)} %copy-done.10), custom_call_target="tpu_custom_call" | custom-call | flops 1000000 | bytes 100000 | tf_op jit(solution)/shard_map/pallas_call | solution.py:333
  24.5 7.6 %all-to-all-start = ((bf16[32,16,128]{2,1,0:T(8,128)(2,1)}), bf16[32,16,128]{2,1,0:T(8,128)(2,1)S(1)}, u32[]{:S(2)}, u32[]{:S(2)}) async-start(bf16[32,16,128]{2,1,0:T(8,128)(2,1)} %get-tuple-element.13), calls=%async_computation | async-start | bytes 262144 | tf_op jit(solution)/shard_map/all_to_all | solution.py:339
  32.1 0.0 copy-start.4
  32.1 0.1 pad_dynamic-update-slice_fusion.4
  32.3 0.5 concatenate.6
  32.8 0.8 pad.86
  33.5 0.0 copy-done.4
  33.6 0.2 copy.18
  33.7 0.2 reshape.49
  33.9 0.1 pad_dynamic-update-slice_fusion.2
  34.0 0.1 pad_dynamic-update-slice_fusion.1
  34.1 0.1 pad_dynamic-update-slice_fusion.t2
  34.3 0.0 copy-start
  34.3 6.7 %all-to-all-done.slots = bf16[32,16,128]{2,1,0:T(8,128)(2,1)S(1)} async-done(((bf16[32,16,128]{2,1,0:T(8,128)(2,1)}), bf16[32,16,128]{2,1,0:T(8,128)(2,1)S(1)}, u32[]{:S(2)}, u32[]{:S(2)}) %all-to-all-start) | async-done | bytes 131104 | tf_op jit(solution)/shard_map/all_to_all | solution.py:339
  41.0 0.0 copy-done
  41.0 0.7 copy-done.1
  41.6 8.2 %shard_map.142 = bf16[32,8,128]{2,1,0:T(8,128)(2,1)} custom-call(bf16[64,128]{1,0:T(8,128)(2,1)} %get-tuple-element.12.block, bf16[32,16,128]{2,1,0:T(8,128)(2,1)} %copy-done.1, bf16[384,512]{1,0:T(8,128)(2,1)} %bitcast.23, f32[1,32]{1,0:T(1,128)} %bitcast.36, bf16[9,256,256]{2,1,0:T(8,128)(2,1)} %copy-done, f32[1,32]{1,0:T(1,128)} %bitcast.37, ...), custom_call_target="tpu_custom_call" | custom-call | flops 10000000 | bytes 100000 | tf_op jit(solution)/shard_map/pallas_call | solution.py:344
  49.8 3.9 %all-to-all-start.1 = ((bf16[32,8,128]{2,1,0:T(8,128)(2,1)}), bf16[32,8,128]{2,1,0:T(8,128)(2,1)S(1)}, u32[]{:S(2)}, u32[]{:S(2)}) async-start(bf16[32,8,128]{2,1,0:T(8,128)(2,1)} %shard_map.142), calls=%async_computation.1 | async-start | bytes 131072 | tf_op jit(solution)/shard_map/all_to_all | solution.py:369
  53.7 0.0 copy-done.5
  53.7 2.1 %collective-permute-start.2 = (bf16[216,256]{1,0:T(8,128)(2,1)S(1)}, bf16[216,256]{1,0:T(8,128)(2,1)S(1)}, u32[]{:S(2)}, u32[]{:S(2)}) collective-permute-start(bf16[216,256]{1,0:T(8,128)(2,1)S(1)} %bitcast.30), channel_id=1, source_target_pairs={{0,16},{16,0},{32,48},{48,32},{64,80},{80,64},{96,112},{112,96},{1... | collective-permute-start | bytes 331784 | tf_op jit(solution)/shard_map/ppermute | solution.py:329
  55.8 2.3 %collective-permute-start.3 = (bf16[216,256]{1,0:T(8,128)(2,1)S(1)}, bf16[216,256]{1,0:T(8,128)(2,1)S(1)}, u32[]{:S(2)}, u32[]{:S(2)}) collective-permute-start(bf16[216,256]{1,0:T(8,128)(2,1)S(1)} %bitcast.32), channel_id=1, source_target_pairs={{0,16},{16,0},{32,48},{48,32},{64,80},{80,64},{96,112},{112,96},{1... | collective-permute-start | bytes 331784 | tf_op jit(solution)/shard_map/ppermute | solution.py:329
  58.1 0.0 collective-permute-done.2.w_far
  58.1 0.0 copy-start.7
  58.1 0.9 %collective-permute-done.3.p_far = bf16[216,256]{1,0:T(8,128)(2,1)S(1)} collective-permute-done((bf16[216,256]{1,0:T(8,128)(2,1)S(1)}, bf16[216,256]{1,0:T(8,128)(2,1)S(1)}, u32[]{:S(2)}, u32[]{:S(2)}) %collective-permute-start.3) | collective-permute-done | bytes 110624 | tf_op jit(solution)/shard_map/ppermute | solution.py:329
  59.0 2.7 %all-to-all-done.1.got = bf16[32,8,128]{2,1,0:T(8,128)(2,1)S(1)} async-done(((bf16[32,8,128]{2,1,0:T(8,128)(2,1)}), bf16[32,8,128]{2,1,0:T(8,128)(2,1)S(1)}, u32[]{:S(2)}, u32[]{:S(2)}) %all-to-all-start.1) | async-done | bytes 65568 | tf_op jit(solution)/shard_map/all_to_all | solution.py:369
  61.7 0.0 copy-done.8
  61.7 0.6 copy-done.2
  62.3 3.0 %shard_map.143 = bf16[16,16,512]{2,1,0:T(8,128)(2,1)} custom-call(bf16[32,8,128]{2,1,0:T(8,128)(2,1)} %copy-done.2, bf16[216,256]{1,0:T(8,128)(2,1)} %bitcast.29, bf16[216,256]{1,0:T(8,128)(2,1)} %bitcast.31, bf16[216,256]{1,0:T(8,128)(2,1)} %copy-done.7, bf16[216,256]{1,0:T(8,128)(2,1)} %copy-done.8), custom_call_target="tpu_custom_call" | custom-call | flops 10000000 | bytes 100000 | tf_op jit(solution)/shard_map/pallas_call | solution.py:370
  65.4 16.8 %all_to_all.15.got = bf16[16,16,512]{2,1,0:T(8,128)(2,1)} all-to-all(bf16[16,16,512]{2,1,0:T(8,128)(2,1)} %shard_map.143), channel_id=1, replica_groups={{0,32,64,96,128,160,192,224,256,288,320,352,384,416,448,480},{16,48,80,..., dimensions={0} | all-to-all | bytes 524288 | tf_op jit(solution)/shard_map/all_to_all | solution.py:378
  82.2 1.9 %shard_map.144 = (bf16[8,8,4,16]{3,2,1,0:T(4,128)(2,1)}, bf16[8,8,4,16]{3,2,1,0:T(4,128)(2,1)}) custom-call(bf16[16,16,512]{2,1,0:T(8,128)(2,1)} %all_to_all.15.got, f32[8]{0:T(128)} %bias.1), custom_call_target="tpu_custom_call" | custom-call | flops 1000000 | bytes 100000 | tf_op jit(solution)/shard_map/pallas_call | solution.py:381
  (11 shorter events, 0.1 us)
Async XLA Ops:
  0.6 18.3 %copy-start.3 = (bf16[32,3,3,3,32]{4,0,3,2,1:T(8,128)(2,1)S(1)}, bf16[32,3,3,3,32]{4,0,3,2,1:T(8,128)(2,1)}, u32[]{:S(2)}) copy-start(bf16[32,3,3,3,32]{4,0,3,2,1:T(8,128)(2,1)} %param.17) | copy-start | bytes 165892
  2.3 17.2 %collective-permute-start = (bf16[16,128]{1,0:T(8,128)(2,1)}, bf16[16,128]{1,0:T(8,128)(2,1)S(1)}, u32[]{:S(2)}, u32[]{:S(2)}) collective-permute-start(bf16[16,128]{1,0:T(8,128)(2,1)} %get-tuple-element.10), channel_id=1, source_target_pairs={{0,1},{1,2},{2,3},{3,4},{4,5},{5,6},{6,7},{7,8},{8,9},{9,10},{10,1... | collective-permute-start | bytes 12296 | tf_op jit(solution)/shard_map/ppermute | solution.py:321
  11.4 10.9 %collective-permute-start.1 = (bf16[16,128]{1,0:T(8,128)(2,1)}, bf16[16,128]{1,0:T(8,128)(2,1)S(1)}, u32[]{:S(2)}, u32[]{:S(2)}) collective-permute-start(bf16[16,128]{1,0:T(8,128)(2,1)} %get-tuple-element.11), channel_id=1, source_target_pairs={{1,0},{2,1},{3,2},{4,3},{5,4},{6,5},{7,6},{8,7},{9,8},{10,9},{11,1... | collective-permute-start | bytes 12296 | tf_op jit(solution)/shard_map/ppermute | solution.py:322
  19.6 2.8 %copy-start.9 = (bf16[16,128]{1,0:T(8,128)(2,1)}, bf16[16,128]{1,0:T(8,128)(2,1)S(1)}, u32[]{:S(2)}) copy-start(bf16[16,128]{1,0:T(8,128)(2,1)S(1)} %collective-permute-done.left) | copy-start | bytes 12292
  22.3 0.6 copy-start.10
  24.5 16.5 %all-to-all-start = ((bf16[32,16,128]{2,1,0:T(8,128)(2,1)}), bf16[32,16,128]{2,1,0:T(8,128)(2,1)S(1)}, u32[]{:S(2)}, u32[]{:S(2)}) async-start(bf16[32,16,128]{2,1,0:T(8,128)(2,1)} %get-tuple-element.13), calls=%async_computation | async-start | bytes 262144 | tf_op jit(solution)/shard_map/all_to_all | solution.py:339
  32.1 1.4 %copy-start.4 = (bf16[32,3,3,3,32]{4,0,3,2,1:T(8,128)(2,1)S(1)}, bf16[32,3,3,3,32]{4,0,3,2,1:T(8,128)(2,1)}, u32[]{:S(2)}) copy-start(bf16[32,3,3,3,32]{4,0,3,2,1:T(8,128)(2,1)} %param.19) | copy-start | bytes 165892
  34.3 6.7 %copy-start = (bf16[9,256,256]{2,1,0:T(8,128)(2,1)}, bf16[9,256,256]{2,1,0:T(8,128)(2,1)S(1)}, u32[]{:S(2)}) copy-start(bf16[9,256,256]{2,1,0:T(8,128)(2,1)S(1)} %pad_dynamic-update-slice_fusion.t2) | copy-start | bytes 3538948
  41.0 0.7 copy-start.1
  41.6 12.1 %copy-start.5 = (bf16[256,3,3,3,8]{0,4,3,2,1:T(8,128)(2,1)S(1)}, bf16[256,3,3,3,8]{0,4,3,2,1:T(8,128)(2,1)}, u32[]{:S(2)}) copy-start(bf16[256,3,3,3,8]{0,4,3,2,1:T(8,128)(2,1)} %param.23) | copy-start | bytes 331780
  41.6 14.2 %copy-start.6 = (bf16[256,3,3,3,8]{0,4,3,2,1:T(8,128)(2,1)S(1)}, bf16[256,3,3,3,8]{0,4,3,2,1:T(8,128)(2,1)}, u32[]{:S(2)}) copy-start(bf16[256,3,3,3,8]{0,4,3,2,1:T(8,128)(2,1)} %param.25) | copy-start | bytes 331780
  49.8 11.9 %all-to-all-start.1 = ((bf16[32,8,128]{2,1,0:T(8,128)(2,1)}), bf16[32,8,128]{2,1,0:T(8,128)(2,1)S(1)}, u32[]{:S(2)}, u32[]{:S(2)}) async-start(bf16[32,8,128]{2,1,0:T(8,128)(2,1)} %shard_map.142), calls=%async_computation.1 | async-start | bytes 131072 | tf_op jit(solution)/shard_map/all_to_all | solution.py:369
  53.7 4.4 %collective-permute-start.2 = (bf16[216,256]{1,0:T(8,128)(2,1)S(1)}, bf16[216,256]{1,0:T(8,128)(2,1)S(1)}, u32[]{:S(2)}, u32[]{:S(2)}) collective-permute-start(bf16[216,256]{1,0:T(8,128)(2,1)S(1)} %bitcast.30), channel_id=1, source_target_pairs={{0,16},{16,0},{32,48},{48,32},{64,80},{80,64},{96,112},{112,96},{1... | collective-permute-start | bytes 331784 | tf_op jit(solution)/shard_map/ppermute | solution.py:329
  55.8 3.2 %collective-permute-start.3 = (bf16[216,256]{1,0:T(8,128)(2,1)S(1)}, bf16[216,256]{1,0:T(8,128)(2,1)S(1)}, u32[]{:S(2)}, u32[]{:S(2)}) collective-permute-start(bf16[216,256]{1,0:T(8,128)(2,1)S(1)} %bitcast.32), channel_id=1, source_target_pairs={{0,16},{16,0},{32,48},{48,32},{64,80},{80,64},{96,112},{112,96},{1... | collective-permute-start | bytes 331784 | tf_op jit(solution)/shard_map/ppermute | solution.py:329
  58.1 3.6 %copy-start.7 = (bf16[216,256]{1,0:T(8,128)(2,1)}, bf16[216,256]{1,0:T(8,128)(2,1)S(1)}, u32[]{:S(2)}) copy-start(bf16[216,256]{1,0:T(8,128)(2,1)S(1)} %collective-permute-done.2.w_far) | copy-start | bytes 331780
  59.0 2.7 %copy-start.8 = (bf16[216,256]{1,0:T(8,128)(2,1)}, bf16[216,256]{1,0:T(8,128)(2,1)S(1)}, u32[]{:S(2)}) copy-start(bf16[216,256]{1,0:T(8,128)(2,1)S(1)} %collective-permute-done.3.p_far) | copy-start | bytes 331780
  61.7 0.6 copy-start.2

commit v2 on v1

v2 whole, which is shorter than its diff:
```python
import jax
import jax.numpy as jnp
from jax import lax
from jax.experimental import pallas as pl
from jax.experimental.pallas import tpu as pltpu
from jax.sharding import PartitionSpec as P


BF = jnp.bfloat16
F32 = jnp.float32
VM = pl.BlockSpec(memory_space=pltpu.VMEM)
SM = pl.BlockSpec(memory_space=pltpu.SMEM)


def call(kernel, outs, scratch=(), specs=None, flops=1000000, mib=4):
    return pl.pallas_call(
        kernel,
        out_shape=outs,
        in_specs=specs,
        out_specs=jax.tree.map(lambda _: VM, outs),
        scratch_shapes=list(scratch),
        cost_estimate=pl.CostEstimate(flops=flops, bytes_accessed=100000, transcendentals=0),
        compiler_params=pltpu.CompilerParams(vmem_limit_bytes=mib << 20),
    )


def silu_pair(v, direction):
    s = 1.0 / (1.0 + jnp.exp(-v))
    return v * s, s * (1.0 + v * (1.0 - s)) * direction


def iota(shape, dim):
    return lax.broadcasted_iota(jnp.int32, shape, dim)


SIDES = [(dx, dy) for dx in (-1, 0, 1) for dy in (-1, 0, 1) if dx or dy]


def inside(dx, dy):
    sx, sy = lax.axis_index("sx") + dx, lax.axis_index("sy") + dy
    ok = (sx >= 0) & (sx < 4) & (sy >= 0) & (sy < 8)
    return ok, jnp.where(ok, sx * 8 + sy, 0)


def face_kernel(dens, own, slots, cells):
    total = jnp.zeros((64, 64), F32)
    for c in range(4):
        rows = dens[c].astype(F32).reshape(64, 16).astype(BF)
        place = (iota((16, 64), 1) == 4 * iota((16, 64), 0) + c).astype(BF)
        total += jnp.dot(rows, place, preferred_element_type=F32)
    own[...] = total.astype(BF)
    cells[...] = jnp.concatenate([total, total], axis=1)
    slots[...] = jnp.zeros_like(slots)
    low = iota((8, 128), 1) < 64
    for dx, dy in SIDES:
        ok, at = inside(dx, dy)

        @pl.when(ok)
        def _(dx=dx, dy=dy, at=at):
            x, y = (6 if dx > 0 else 0), (6 if dy > 0 else 0)
            if dx == 0:
                near, far = cells[pl.ds(y, 8, stride=8), :], cells[pl.ds(y + 1, 8, stride=8), :]
            else:
                near, far = cells[8 * x : 8 * x + 8, :], cells[8 * x + 8 : 8 * x + 16, :]
            slots[at] = jnp.where(low, near, far).astype(BF)


def tile_kernel(own, slots, tile, to_right, to_left, dens):
    dens[...] = jnp.zeros_like(dens)
    cells = own[...].astype(F32)
    for x in range(8):
        dens[2 + x, 2:10, :] = cells[8 * x : 8 * x + 8]
    for dx, dy in SIDES:
        ok, at = inside(dx, dy)

        @pl.when(ok)
        def _(dx=dx, dy=dy, at=at):
            got = slots[at].astype(F32)
            x, y = (10 if dx > 0 else 0), (10 if dy > 0 else 0)
            for j in range(2):
                half = got[:, 64 * j : 64 * j + 64]
                if dx == 0:
                    for i in range(8):
                        dens[2 + i, y + j : y + j + 1, :] = half[i : i + 1]
                elif dy == 0:
                    dens[x + j, 2:10, :] = half
                else:
                    row = 0 if dy > 0 else 6
                    dens[x + j, y : y + 2, :] = half[row : row + 2]

    rows = dens[...].reshape(192, 64)
    tile[...] = rows.astype(BF)
    for ref, at in ((to_right, 32), (to_left, 0)):
        ref[...] = jnp.concatenate(
            [rows[48 * g : 48 * g + 48, at : at + 32] for g in range(4)], axis=1
        ).astype(BF)


def lift_kernel(
    tile, right, left, t1, w2, lift_w, lift_p, biases, out, dens, win, acc1, hp, t2, acc2, lhs
):
    def unpack(ref):
        v = ref[...].astype(F32)
        return jnp.concatenate([v[:, 32 * g : 32 * g + 32] for g in range(4)], axis=0)

    dens[...] = jnp.concatenate(
        [unpack(left), tile[...].astype(F32), unpack(right)], axis=1
    ).reshape(12, 16, 128)
    wide = iota((32, 128), 1)
    for t in range(9):
        for i in range(2):
            v = w2[t, 32 * i : 32 * i + 32].astype(F32)
            for z in range(4):
                moved = v if z == 0 else pltpu.roll(v, 32 * z, 1)
                at = slice(128 * i + 32 * z, 128 * i + 32 * z + 32)
                t2[t, at, 0:128] = jnp.where(wide >= 32 * z, moved, 0.0).astype(BF)
                t2[t, at, 128:256] = jnp.where(wide < 32 * z, moved, 0.0).astype(BF)

    lane = iota((8, 128), 1)

    def windows(x, carry):
        shifted = []
        for y in range(12):
            row = jnp.broadcast_to(dens[x, y : y + 1, :], (8, 128))
            first = pltpu.roll(row, 8, 1, stride=16, stride_axis=0)
            shifted.append((first, pltpu.roll(first, 32, 1), pltpu.roll(first, 64, 1)))
        for y in range(10):
            win[x, 8 * y : 8 * y + 8, :] = jnp.where(
                lane < 32, shifted[y][0], jnp.where(lane < 64, shifted[y + 1][1], shifted[y + 2][2])
            )
        return carry

    lax.fori_loop(0, 12, windows, 0)

    rows = jnp.concatenate(
        [win[p : p + 10].reshape(800, 128).astype(BF) for p in range(3)], axis=1
    )
    acc1[...] = jnp.dot(rows, t1[...], preferred_element_type=F32)

    fine = 16 * lax.axis_index("sz") + 4 * (6 - iota((8, 256), 0)) - 1 + iota((8, 256), 1) // 32
    zmask = jnp.where((fine >= 0) & (fine < 256), 1.0, 0.0)
    bias3, bias1, bias2 = biases[:, 0:256], biases[:, 256:512], biases[:, 512:640]

    def first(x, carry):
        gx = 8 * lax.axis_index("sx") + x - 1
        okx = (gx >= 0) & (gx < 32)
        for y in range(10):
            gy = 8 * lax.axis_index("sy") + y - 1
            ok = okx & (gy >= 0) & (gy < 64)
            mask = jnp.where(ok, zmask, 0.0)
            at = pl.ds(pl.multiple_of(80 * x + 8 * y, 8), 8)
            h, d = silu_pair(acc1[at, 0:256] + bias1, acc1[at, 256:512])
            hp[x, y] = jnp.concatenate([h * mask, d * mask], axis=0).astype(BF)
        return carry

    lax.fori_loop(0, 10, first, 0)

    for t in range(9):
        p, q = divmod(t, 3)
        part = lax.dot_general(
            hp[p : p + 8, q : q + 8].reshape(1024, 256),
            t2[t],
            (((1,), (1,)), ((), ())),
            preferred_element_type=F32,
        )
        if t == 0:
            acc2[...] = part
        else:
            acc2[...] += part

    for x in range(8):
        for y in range(8):
            r = 16 * (8 * x + y)
            h, d = silu_pair(
                acc2[r : r + 8, 0:128] + bias2,
                acc2[r : r + 8, 128:256] + acc2[r + 8 : r + 16, 0:128],
            )
            at = 16 * (2 * (x // 4) + y // 4)
            tap = 128 * (4 * (x % 4) + y % 4)
            lhs[at : at + 16, tap : tap + 128] = jnp.concatenate([h, d], axis=0).astype(BF)

    taps = lhs[...]
    by_w = jnp.dot(taps, lift_w[...], preferred_element_type=F32)
    by_p = jnp.dot(taps, lift_p[...], preferred_element_type=F32)
    level = 7 - iota((8, 256), 0)
    coarse = 4 * lax.axis_index("sz") + level - 1
    mask = jnp.where((level < 6) & (coarse >= 0) & (coarse < 64), 1.0, 0.0)
    hs, ds = [], []
    for k in range(4):
        h, d = silu_pair(
            by_w[16 * k : 16 * k + 8] + bias3,
            by_p[16 * k : 16 * k + 8] + by_w[16 * k + 8 : 16 * k + 16],
        )
        hs.append(h * mask)
        ds.append(d * mask)
    turned = jnp.concatenate(hs + ds, axis=0).T
    for d in range(32):
        four = [turned[8 * (d % 8 + 8 * t) : 8 * (d % 8 + 8 * t) + 8] for t in range(4)]
        out[d] = jnp.concatenate(
            [jnp.concatenate(four[0::2], axis=0), jnp.concatenate(four[1::2], axis=0)], axis=1
        ).astype(BF)


def share_kernel(w, p, out):
    for x in range(4):
        at = slice(64 * x, 64 * x + 64)
        out[x] = jnp.concatenate([w[:, at].astype(F32), p[:, at].astype(F32)], axis=1).astype(BF)


def last_kernel(got, weights, out, flat, turned, pre, dot):
    for g in range(2):
        flat[g] = got[:, 8 * g : 8 * g + 8, :].astype(F32).reshape(256, 128)
        for c in range(8):
            turned[g, pl.ds(c, 128, stride=8), 0:32] = flat[g, pl.ds(c, 32, stride=8), :].T
    lane = iota((8, 128), 1)
    cx, cy, bx, by = lane >> 6, (lane >> 5) & 1, (lane >> 3) & 3, lane & 7

    def shift_x(v, by_one):
        if by_one == 0:
            return v
        if by_one > 0:
            s = jnp.where(cx == 0, pltpu.roll(v, 64, 1), pltpu.roll(v, 56, 1))
            return jnp.where((cx == 1) & (bx == 3), 0.0, s)
        s = jnp.where(cx == 1, pltpu.roll(v, 64, 1), pltpu.roll(v, 72, 1))
        return jnp.where((cx == 0) & (bx == 0), 0.0, s)

    def shift_y(v, by_one):
        if by_one == 0:
            return v
        if by_one > 0:
            s = jnp.where(cy == 0, pltpu.roll(v, 96, 1), pltpu.roll(v, 31, 1))
            return jnp.where((cy == 1) & (by == 7), 0.0, s)
        s = jnp.where(cy == 1, pltpu.roll(v, 32, 1), pltpu.roll(v, 97, 1))
        return jnp.where((cy == 0) & (by == 0), 0.0, s)

    def columns(k, kind):
        pieces = {}
        for z in range(6):
            tile = jnp.concatenate(
                [
                    turned[k // 2, pl.ds(pl.multiple_of(512 * (k % 2) + 8 * (32 * kind + 8 * xy + 7 - z), 8), 8), 0:32]
                    for xy in range(4)
                ],
                axis=1,
            )
            for p in range(3):
                moved = shift_x(tile, p - 1)
                for q in range(3):
                    pieces[p, q, z] = shift_y(moved, q - 1)
        return jnp.concatenate(
            [
                jnp.concatenate([pieces[p, q, r + z] for z in range(4)], axis=1)
                for p in range(3)
                for q in range(3)
                for r in range(3)
            ],
            axis=0,
        ).astype(BF)

    def product(w, x):
        return lax.dot_general(w, x, (((0,), (0,)), ((), ())), preferred_element_type=F32)

    pre[...] = jnp.zeros_like(pre)
    dot[...] = jnp.zeros_like(dot)

    def add(k, carry):
        by_h = product(weights[k], columns(k, 0))
        pre[...] += by_h[0:64]
        dot[...] += by_h[64:128] + product(weights[k], columns(k, 1))[0:64]
        return carry

    lax.fori_loop(0, 4, add, 0)
    out[...] = jnp.concatenate(
        [pre[...].reshape(8, 8, 512), dot[...].reshape(8, 8, 512)], axis=1
    ).astype(BF)


def sum_kernel(got, bias, features, tangent, rows):
    total = got[0].astype(F32)
    for s in range(1, 8):
        total = total + got[s].astype(F32)
    level = iota((16, 512), 0)
    for o in range(8):
        total = total + jnp.where(level == o, bias[o], 0.0)
    total = total.astype(BF)
    here, there = iota((128, 128), 0), iota((128, 128), 1)
    gx = 2 * ((here >> 3) & 3) + (here >> 6)
    gy = 2 * (here & 7) + ((here >> 5) & 1)
    place = (there == 16 * gx + gy).astype(BF)
    for z in range(4):
        rows[pl.ds(z, 16, stride=4), :] = jnp.dot(
            total[:, 128 * z : 128 * z + 128], place, preferred_element_type=F32
        )
    for x in range(8):
        moved = rows[...] if x == 0 else pltpu.roll(rows[...], 128 - 16 * x, 1)
        for o in range(8):
            features[o, x] = moved[4 * o : 4 * o + 4, 0:16].astype(BF)
            tangent[o, x] = moved[32 + 4 * o : 32 + 4 * o + 4, 0:16].astype(BF)


def first_matrix(w, p):
    def bands(v):
        v = jnp.transpose(v, (1, 2, 3, 4, 0)).reshape(3, 3, 12, 32)
        wide = [jnp.pad(v, ((0, 0), (0, 0), (4 * z, 20 - 4 * z), (0, 0))) for z in range(6)]
        return jnp.concatenate(wide + [jnp.zeros((3, 3, 32, 64), BF)], axis=3)

    both = jnp.concatenate([bands(w), bands(p)], axis=3).reshape(3, 96, 512)
    return jnp.pad(both, ((0, 0), (0, 32), (0, 0))).reshape(384, 512)


def second_rows(w, p):
    def rows(v):
        return jnp.pad(jnp.transpose(v, (1, 2, 0, 3, 4)).reshape(9, 32, 96), ((0, 0), (0, 0), (0, 32)))

    return jnp.concatenate([rows(w), rows(p)], axis=1)


def body(
    density,
    conv1_weight,
    conv1_bias,
    conv1_probe,
    conv2_weight,
    conv2_bias,
    conv2_probe,
    lift_weight,
    lift_bias,
    lift_probe,
    conv3_weight,
    conv3_bias,
    conv3_probe,
):
    S = jax.ShapeDtypeStruct
    own, faces = call(
        face_kernel,
        (S((64, 64), BF), S((32, 8, 128), BF)),
        scratch=[pltpu.VMEM((64, 128), F32)],
        specs=[VM],
    )(density)
    near = lax.all_to_all(faces, ("sx", "sy"), 0, 0, tiled=True)
    tile, to_right, to_left = call(
        tile_kernel,
        (S((192, 64), BF), S((48, 128), BF), S((48, 128), BF)),
        scratch=[pltpu.VMEM((12, 16, 64), F32)],
        specs=[VM, VM],
    )(own, near)
    from_right = lax.ppermute(to_left, "sz", [(i + 1, i) for i in range(15)])
    from_left = lax.ppermute(to_right, "sz", [(i, i + 1) for i in range(15)])

    def flat3(v):
        return jnp.transpose(v, (1, 2, 3, 4, 0)).reshape(216, 256)

    share = call(share_kernel, S((4, 216, 128), BF), specs=[VM, VM])(
        flat3(conv3_weight), flat3(conv3_probe)
    )
    shares = lax.all_to_all(share, "sx", 0, 0, tiled=True)
    t1 = first_matrix(conv1_weight, conv1_probe)
    w2 = second_rows(conv2_weight, conv2_probe)

    biases = jnp.concatenate(
        [lift_bias] + [conv1_bias] * 6 + [jnp.zeros(64, F32)] + [conv2_bias] * 4
    ).reshape(1, 640)

    def flat_lift(v):
        return jnp.transpose(v, (1, 2, 3, 4, 0)).reshape(2048, 256)

    lift = call(
        lift_kernel,
        S((32, 16, 128), BF),
        scratch=[
            pltpu.VMEM((12, 16, 128), F32),
            pltpu.VMEM((12, 80, 128), F32),
            pltpu.VMEM((800, 512), F32),
            pltpu.VMEM((10, 10, 16, 256), BF),
            pltpu.VMEM((9, 256, 256), BF),
            pltpu.VMEM((1024, 256), F32),
            pltpu.VMEM((64, 2048), BF),
        ],
        specs=[VM] * 8,
        flops=10000000,
        mib=24,
    )
    lifted = lift(
        tile,
        from_right,
        from_left,
        t1,
        w2,
        flat_lift(lift_weight),
        flat_lift(lift_probe),
        biases,
    )
    gathered = lax.all_to_all(lifted, ("sx", "sy"), 0, 0, tiled=True)
    parts = call(
        last_kernel,
        S((8, 16, 512), BF),
        scratch=[
            pltpu.VMEM((2, 256, 128), F32),
            pltpu.VMEM((2, 1024, 128), F32),
            pltpu.VMEM((64, 512), F32),
            pltpu.VMEM((64, 512), F32),
        ],
        specs=[VM] * 2,
        flops=10000000,
        mib=16,
    )(gathered, shares)
    mine = lax.all_to_all(parts, "sy", 0, 0, tiled=True)
    features, tangent = call(
        sum_kernel,
        (S((8, 8, 4, 16), BF), S((8, 8, 4, 16), BF)),
        scratch=[pltpu.VMEM((64, 128), F32)],
        specs=[VM, SM],
    )(mine, conv3_bias)
    return jnp.transpose(features, (0, 1, 3, 2)), jnp.transpose(tangent, (0, 1, 3, 2))


def solution(mesh):
    placed = (
        P(None, "sx", "sy", "sz"),
        P(),
        P(),
        P(),
        P(),
        P(),
        P(),
        P(),
        P(),
        P(),
        P(None, None, None, None, ("sx", "sy")),
        P(("sx", "sy")),
        P(None, None, None, None, ("sx", "sy")),
    )

    return jax.shard_map(
        body,
        mesh=mesh,
        in_specs=placed,
        out_specs=(P(("sx", "sy"), None, None, "sz"), P(("sx", "sy"), None, None, "sz")),
        check_vma=False,
    )
```

time: 84.8 us -> 80.1 us (0.945)
  blocking collectives: 16.8 us -> 23.7 us
  starting transfers between devices: 30.7 us -> 24.7 us
  Pallas kernels: 16.4 us -> 11.6 us
    ppermute x1, starting transfers between devices: 9.08 us -> 1.92 us  [body(): from_left = lax.ppermute(to_right, 'sz', [(i, i + 1) for i in range(15)])]
    all_to_all x1 -> x2, blocking collectives: 16.8 us -> 23.7 us  [the longest x1 14.5 us: body(): gathered = lax.all_to_all(lifted, ('sx', 'sy'), 0, 0, tiled=True)]
    ppermute x1, waiting for transfers between devices: 0.01 us -> 6.01 us  [body(): from_left = lax.ppermute(to_right, 'sz', [(i, i + 1) for i in range(15)])]
    ppermute x1, starting transfers between devices: 5.82 us -> 10.3 us  [body(): from_right = lax.ppermute(to_left, 'sz', [(i + 1, i) for i in range(15)])]
    pallas_call x4 -> x5, Pallas kernels: 14.5 us -> 10.1 us  [the longest x1 5.66 us: body(): lift(tile, from_right, from_left, t1, w2, flat_lift(lift_weight), flat_li...]
    ppermute x2 -> x0, starting transfers between devices: 4.33 us -> none  [the longest x1 2.26 us: body(): lax.ppermute(p3, 'sy', swap)]
    all_to_all x2, waiting for transfers between devices: 9.37 us -> 6.33 us  [the longest x1 6.33 us: body(): near = lax.all_to_all(faces, ('sx', 'sy'), 0, 0, tiled=True)]
    ppermute x1, waiting for transfers between devices: 2.74 us -> 0.01 us  [body(): from_right = lax.ppermute(to_left, 'sz', [(i + 1, i) for i in range(15)])]
  transfers between devices with their start and end apart: 6 -> 4, of which waited for: 4 -> 2; matrix products, arithmetic and copies ran while one was open for 5% -> 5% of each run, Pallas kernels for 0% -> 9%
where the time goes in v2:
time: 80.1 us; the launch traced here: 79.6 us
  starting transfers between devices  24.7 us (31%)
  blocking collectives  23.7 us (30%)
  waiting for transfers between devices  12.3 us (15%)
  Pallas kernels  11.6 us (14%)
  local copies, waits for them, and re-layouts  6.37 us (8%)
  between operations  0.93 us (1%)
    all_to_all x1, blocking collectives, body(): gathered = lax.all_to_all(lifted, ('sx', 'sy'), 0, 0, tiled=True)  14.5 us
    ppermute x1, starting transfers between devices, body(): from_right = lax.ppermute(to_left, 'sz', [(i + 1, i) for i in range(15)])  10.3 us
    all_to_all x1, blocking collectives, body(): mine = lax.all_to_all(parts, 'sy', 0, 0, tiled=True)  9.14 us
    all_to_all x1, starting transfers between devices, body(): near = lax.all_to_all(faces, ('sx', 'sy'), 0, 0, tiled=True)  9.07 us
    all_to_all x1, waiting for transfers between devices, body(): near = lax.all_to_all(faces, ('sx', 'sy'), 0, 0, tiled=True)  6.33 us
    ppermute x1, waiting for transfers between devices, body(): from_left = lax.ppermute(to_right, 'sz', [(i, i + 1) for i in range(15)])  6.01 us
    pallas_call x1, Pallas kernels, body(): lift(tile, from_right, from_left, t1, w2, flat_lift(lift_weight), flat_li...  5.66 us
    all_to_all x1, starting transfers between devices, body(): shares = lax.all_to_all(share, 'sx', 0, 0, tiled=True)  3.38 us
  transfers between devices with their start and end apart: 4, of which 2 were waited for; matrix products, arithmetic and copies ran while one was open for 5% of the time, Pallas kernels for 9%

profile of v2, /device:TPU:6, one launch (start us, length us, event | category | flops | bytes accessed | tf_op | source)
XLA Modules:
  0.0 79.6 jit_solution(13377116799701176059)
XLA Ops:
  0.6 0.0 copy-start.4
  0.6 0.8 %copy-done.4 = bf16[4,8,8,16]{3,2,1,0:T(8,128)(2,1)S(1)} copy-done((bf16[4,8,8,16]{3,2,1,0:T(8,128)(2,1)S(1)}, bf16[4,8,8,16]{3,2,1,0:T(8,128)(2,1)}, u32[]{:S(2)}) %copy-start.4) | copy-done | bytes 8216
  1.5 0.9 %shard_map.140 = (bf16[64,64]{1,0:T(8,128)(2,1)S(1)}, bf16[32,8,128]{2,1,0:T(8,128)(2,1)}) custom-call(bf16[4,8,8,16]{3,2,1,0:T(8,128)(2,1)S(1)} %copy-done.4), custom_call_target="tpu_custom_call" | custom-call | flops 1000000 | bytes 100000 | tf_op jit(solution)/shard_map/pallas_call | solution.py:334
  2.3 9.1 %all-to-all-start = ((bf16[32,8,128]{2,1,0:T(8,128)(2,1)}), bf16[32,8,128]{2,1,0:T(8,128)(2,1)S(1)}, u32[]{:S(2)}, u32[]{:S(2)}) async-start(bf16[32,8,128]{2,1,0:T(8,128)(2,1)} %get-tuple-element.10), calls=%async_computation | async-start | bytes 131072 | tf_op jit(solution)/shard_map/all_to_all | solution.py:340
  11.4 0.0 copy-done.12
  11.5 0.0 copy-done.13
  11.5 0.0 copy-done.2
  11.5 0.0 copy-done.3
  11.5 0.8 %shard_map.143 = bf16[4,216,128]{2,1,0:T(8,128)(2,1)} custom-call(bf16[216,256]{1,0:T(8,128)(2,1)S(1)} %bitcast.23, bf16[216,256]{1,0:T(8,128)(2,1)S(1)} %bitcast.24), custom_call_target="tpu_custom_call" | custom-call | flops 1000000 | bytes 100000 | tf_op jit(solution)/shard_map/pallas_call | solution.py:353
  12.3 0.8 fusion.3
  13.1 6.3 %all-to-all-done.slots = bf16[32,8,128]{2,1,0:T(8,128)(2,1)S(1)} async-done(((bf16[32,8,128]{2,1,0:T(8,128)(2,1)}), bf16[32,8,128]{2,1,0:T(8,128)(2,1)S(1)}, u32[]{:S(2)}, u32[]{:S(2)}) %all-to-all-start) | async-done | bytes 65568 | tf_op jit(solution)/shard_map/all_to_all | solution.py:340
  19.4 3.4 %all-to-all-start.2 = ((bf16[4,216,128]{2,1,0:T(8,128)(2,1)}), bf16[4,216,128]{2,1,0:T(8,128)(2,1)S(1)}, u32[]{:S(2)}, u32[]{:S(2)}) async-start(bf16[4,216,128]{2,1,0:T(8,128)(2,1)} %shard_map.143), calls=%async_computation.2 | async-start | bytes 442368 | tf_op jit(solution)/shard_map/all_to_all | solution.py:356
  22.8 0.0 copy-start.10
  22.8 0.8 %fusion.4 = (bf16[3,3,32,32]{3,2,1,0:T(8,128)(2,1)}, bf16[3,3,32,32]{3,2,1,0:T(8,128)(2,1)}, bf16[3,3,32,32]{3,2,1,0:T(8,128)(2,1)}, bf16[3,3,32,32]{3,2,1,0:T(8...) fusion(bf16[3,3,12,32]{3,2,1,0:T(8,128)(2,1)S(1)} %reshape.37), kind=kLoop, calls=%fused_computation.6 | loop fusion | bytes 117504 | tf_op jit(solution)/shard_map/jit(_pad)/pad | solution.py:304
  23.6 0.2 copy-done.10
  23.8 0.2 copy.17
  24.0 0.0 copy-start.11
  24.0 0.2 reshape.41
  24.2 0.8 copy-done.11
  24.9 0.2 copy.18
  25.1 0.2 reshape.42
  25.3 0.3 shard_map.141
  25.6 10.3 %collective-permute-start = (bf16[48,128]{1,0:T(8,128)(2,1)S(1)}, bf16[48,128]{1,0:T(8,128)(2,1)S(1)}, u32[]{:S(2)}, u32[]{:S(2)}) collective-permute-start(bf16[48,128]{1,0:T(8,128)(2,1)S(1)} %get-tuple-element.12), channel_id=1, source_target_pairs={{1,0},{2,1},{3,2},{4,3},{5,4},{6,5},{7,6},{8,7},{9,8},{10,9},{11,1... | collective-permute-start | bytes 36872 | tf_op jit(solution)/shard_map/ppermute | solution.py:347
  35.9 1.9 %collective-permute-start.1 = (bf16[48,128]{1,0:T(8,128)(2,1)S(1)}, bf16[48,128]{1,0:T(8,128)(2,1)S(1)}, u32[]{:S(2)}, u32[]{:S(2)}) collective-permute-start(bf16[48,128]{1,0:T(8,128)(2,1)S(1)} %get-tuple-element.13), channel_id=1, source_target_pairs={{0,1},{1,2},{2,3},{3,4},{4,5},{5,6},{6,7},{7,8},{8,9},{9,10},{10,1... | collective-permute-start | bytes 36872 | tf_op jit(solution)/shard_map/ppermute | solution.py:348
  37.9 0.0 copy-start.6
  37.9 0.0 copy-start.7
  37.9 0.0 copy-start.8
  37.9 0.0 copy-start.14
  37.9 0.0 copy-start.15
  37.9 0.0 copy-start.16
  38.0 0.0 copy-start
  38.0 0.0 copy-start.1
  38.0 0.7 copy-done.6
  38.7 0.0 copy-done.7
  38.8 0.0 copy-done.8
  38.8 0.0 copy-done.9
  38.9 1.3 %concatenate.9 = bf16[3,3,32,512]{3,2,1,0:T(8,128)(2,1)S(1)} concatenate(bf16[3,3,32,32]{3,2,1,0:T(8,128)(2,1)} %get-tuple-element.27, bf16[3,3,32,32]{3,2,1,0:T(8,128)(2,1)} %get-tuple-element.26, bf16[3,3,32,32]{3,2,1,0:T(8,128)(2,1)} %get-tuple-element.25, bf16[3,3,32,32]{3,2,1,0:T(8,128)(2,1)} %get-tuple-element.24, bf16[3,3,32,32]{3,2,1,0:T(8,128)(2,1)} %get-tuple-element.23, ...), dimensions={3} | concatenate | bytes 589824 | tf_op jit(solution)/shard_map/concatenate | solution.py:307
  40.2 0.1 concatenate.11
  40.3 0.0 collective-permute-done.right
  40.3 6.0 %collective-permute-done.1.left = bf16[48,128]{1,0:T(8,128)(2,1)S(1)} collective-permute-done((bf16[48,128]{1,0:T(8,128)(2,1)S(1)}, bf16[48,128]{1,0:T(8,128)(2,1)S(1)}, u32[]{:S(2)}, u32[]{:S(2)}) %collective-permute-start.1) | collective-permute-done | bytes 12320 | tf_op jit(solution)/shard_map/ppermute | solution.py:348
  46.3 0.0 copy-done.1
  46.3 5.7 %shard_map.142 = bf16[32,16,128]{2,1,0:T(8,128)(2,1)S(1)} custom-call(bf16[192,64]{1,0:T(8,128)(2,1)S(1)} %get-tuple-element.11.tile, bf16[48,128]{1,0:T(8,128)(2,1)S(1)} %collective-permute-done.right, bf16[48,128]{1,0:T(8,128)(2,1)S(1)} %collective-permute-done.1.left, bf16[384,512]{1,0:T(8,128)(2,1)S(1)} %bitcast.20, bf16[9,64,128]{2,1,0:T(8,128)(2,1)S(1)} %fusion.2.w2, ...), custom_call_target="tpu_custom_call" | custom-call | flops 10000000 | bytes 100000 | tf_op jit(solution)/shard_map/pallas_call | solution.py:383
  52.0 0.0 all-to-all-done.2.weights
  52.0 14.5 %all_to_all.20.got = bf16[32,16,128]{2,1,0:T(8,128)(2,1)S(1)} all-to-all(bf16[32,16,128]{2,1,0:T(8,128)(2,1)S(1)} %shard_map.142), channel_id=1, replica_groups=mesh['sx'=4,'sy'=8,'sz'=16] {'sx','sy'}, dimensions={0} | all-to-all | bytes 262144 | tf_op jit(solution)/shard_map/all_to_all | solution.py:393
  66.5 2.4 %shard_map.144 = bf16[8,16,512]{2,1,0:T(8,128)(2,1)S(1)} custom-call(bf16[32,16,128]{2,1,0:T(8,128)(2,1)S(1)} %all_to_all.20.got, bf16[4,216,128]{2,1,0:T(8,128)(2,1)S(1)} %all-to-all-done.2.weights), custom_call_target="tpu_custom_call" | custom-call | flops 10000000 | bytes 100000 | tf_op jit(solution)/shard_map/pallas_call | solution.py:394
  69.0 0.0 copy-start.5
  69.0 9.1 %all_to_all.21.got = bf16[8,16,512]{2,1,0:T(8,128)(2,1)S(1)} all-to-all(bf16[8,16,512]{2,1,0:T(8,128)(2,1)S(1)} %shard_map.144), channel_id=1, replica_groups=mesh['sx'=4,'sy'=8,'sz'=16] {'sy'}, dimensions={0} | all-to-all | bytes 262144 | tf_op jit(solution)/shard_map/all_to_all | solution.py:407
  78.1 1.5 %shard_map.145 = (bf16[8,8,4,16]{3,2,1,0:T(4,128)(2,1)}, bf16[8,8,4,16]{3,2,1,0:T(4,128)(2,1)}) custom-call(bf16[8,16,512]{2,1,0:T(8,128)(2,1)S(1)} %all_to_all.21.got, f32[8]{0:T(128)S(1)} %copy-done.5), custom_call_target="tpu_custom_call" | custom-call | flops 1000000 | bytes 100000 | tf_op jit(solution)/shard_map/pallas_call | solution.py:408
  (17 shorter events, 0.2 us)
Async XLA Ops:
  0.6 0.8 %copy-start.4 = (bf16[4,8,8,16]{3,2,1,0:T(8,128)(2,1)S(1)}, bf16[4,8,8,16]{3,2,1,0:T(8,128)(2,1)}, u32[]{:S(2)}) copy-start(bf16[4,8,8,16]{3,2,1,0:T(8,128)(2,1)} %dens.1) | copy-start | bytes 24580
  1.5 9.9 %copy-start.12 = (bf16[32,3,3,3,4]{0,4,3,2,1:T(4,128)(2,1)S(1)}, bf16[32,3,3,3,4]{0,4,3,2,1:T(4,128)(2,1)}, u32[]{:S(2)}) copy-start(bf16[32,3,3,3,4]{0,4,3,2,1:T(4,128)(2,1)} %param.16) | copy-start | bytes 20740
  1.5 10.0 %copy-start.13 = (bf16[32,3,3,3,4]{0,4,3,2,1:T(4,128)(2,1)S(1)}, bf16[32,3,3,3,4]{0,4,3,2,1:T(4,128)(2,1)}, u32[]{:S(2)}) copy-start(bf16[32,3,3,3,4]{0,4,3,2,1:T(4,128)(2,1)} %param.14) | copy-start | bytes 20740
  2.3 9.2 %copy-start.2 = (bf16[256,3,3,3,8]{0,4,3,2,1:T(8,128)(2,1)S(1)}, bf16[256,3,3,3,8]{0,4,3,2,1:T(8,128)(2,1)}, u32[]{:S(2)}) copy-start(bf16[256,3,3,3,8]{0,4,3,2,1:T(8,128)(2,1)} %param.23) | copy-start | bytes 331780
  2.3 9.2 %copy-start.3 = (bf16[256,3,3,3,8]{0,4,3,2,1:T(8,128)(2,1)S(1)}, bf16[256,3,3,3,8]{0,4,3,2,1:T(8,128)(2,1)}, u32[]{:S(2)}) copy-start(bf16[256,3,3,3,8]{0,4,3,2,1:T(8,128)(2,1)} %param.25) | copy-start | bytes 331780
  2.3 17.1 %all-to-all-start = ((bf16[32,8,128]{2,1,0:T(8,128)(2,1)}), bf16[32,8,128]{2,1,0:T(8,128)(2,1)S(1)}, u32[]{:S(2)}, u32[]{:S(2)}) async-start(bf16[32,8,128]{2,1,0:T(8,128)(2,1)} %get-tuple-element.10), calls=%async_computation | async-start | bytes 131072 | tf_op jit(solution)/shard_map/all_to_all | solution.py:340
  19.4 32.6 %all-to-all-start.2 = ((bf16[4,216,128]{2,1,0:T(8,128)(2,1)}), bf16[4,216,128]{2,1,0:T(8,128)(2,1)S(1)}, u32[]{:S(2)}, u32[]{:S(2)}) async-start(bf16[4,216,128]{2,1,0:T(8,128)(2,1)} %shard_map.143), calls=%async_computation.2 | async-start | bytes 442368 | tf_op jit(solution)/shard_map/all_to_all | solution.py:356
  22.8 1.0 %copy-start.10 = (bf16[32,3,3,3,32]{4,0,3,2,1:T(8,128)(2,1)S(1)}, bf16[32,3,3,3,32]{4,0,3,2,1:T(8,128)(2,1)}, u32[]{:S(2)}) copy-start(bf16[32,3,3,3,32]{4,0,3,2,1:T(8,128)(2,1)} %param.17) | copy-start | bytes 165892
  24.0 0.9 %copy-start.11 = (bf16[32,3,3,3,32]{4,0,3,2,1:T(8,128)(2,1)S(1)}, bf16[32,3,3,3,32]{4,0,3,2,1:T(8,128)(2,1)}, u32[]{:S(2)}) copy-start(bf16[32,3,3,3,32]{4,0,3,2,1:T(8,128)(2,1)} %param.19) | copy-start | bytes 165892
  25.6 14.7 %collective-permute-start = (bf16[48,128]{1,0:T(8,128)(2,1)S(1)}, bf16[48,128]{1,0:T(8,128)(2,1)S(1)}, u32[]{:S(2)}, u32[]{:S(2)}) collective-permute-start(bf16[48,128]{1,0:T(8,128)(2,1)S(1)} %get-tuple-element.12), channel_id=1, source_target_pairs={{1,0},{2,1},{3,2},{4,3},{5,4},{6,5},{7,6},{8,7},{9,8},{10,9},{11,1... | collective-permute-start | bytes 36872 | tf_op jit(solution)/shard_map/ppermute | solution.py:347
  35.9 10.4 %collective-permute-start.1 = (bf16[48,128]{1,0:T(8,128)(2,1)S(1)}, bf16[48,128]{1,0:T(8,128)(2,1)S(1)}, u32[]{:S(2)}, u32[]{:S(2)}) collective-permute-start(bf16[48,128]{1,0:T(8,128)(2,1)S(1)} %get-tuple-element.13), channel_id=1, source_target_pairs={{0,1},{1,2},{2,3},{3,4},{4,5},{5,6},{6,7},{7,8},{8,9},{9,10},{10,1... | collective-permute-start | bytes 36872 | tf_op jit(solution)/shard_map/ppermute | solution.py:348
  37.9 0.9 %copy-start.6 = (bf16[3,3,32,32]{3,2,1,0:T(8,128)(2,1)S(1)}, bf16[3,3,32,32]{3,2,1,0:T(8,128)(2,1)}, u32[]{:S(2)}) copy-start(bf16[3,3,32,32]{3,2,1,0:T(8,128)(2,1)} %get-tuple-element.18) | copy-start | bytes 55300
  37.9 0.9 %copy-start.7 = (bf16[3,3,32,32]{3,2,1,0:T(8,128)(2,1)S(1)}, bf16[3,3,32,32]{3,2,1,0:T(8,128)(2,1)}, u32[]{:S(2)}) copy-start(bf16[3,3,32,32]{3,2,1,0:T(8,128)(2,1)} %get-tuple-element.19) | copy-start | bytes 55300
  37.9 0.9 %copy-start.8 = (bf16[3,3,32,32]{3,2,1,0:T(8,128)(2,1)S(1)}, bf16[3,3,32,32]{3,2,1,0:T(8,128)(2,1)}, u32[]{:S(2)}) copy-start(bf16[3,3,32,32]{3,2,1,0:T(8,128)(2,1)} %get-tuple-element.20) | copy-start | bytes 55300
  37.9 1.0 %copy-start.9 = (bf16[3,3,32,32]{3,2,1,0:T(8,128)(2,1)S(1)}, bf16[3,3,32,32]{3,2,1,0:T(8,128)(2,1)}, u32[]{:S(2)}) copy-start(bf16[3,3,32,32]{3,2,1,0:T(8,128)(2,1)} %get-tuple-element.21) | copy-start | bytes 55300
  37.9 2.3 %copy-start.14 = (f32[32]{0:T(128)S(1)}, f32[32]{0:T(128)}, u32[]{:S(2)}) copy-start(f32[32]{0:T(128)} %param.15) | copy-start | bytes 388
  37.9 2.3 %copy-start.15 = (f32[32]{0:T(128)S(1)}, f32[32]{0:T(128)}, u32[]{:S(2)}) copy-start(f32[32]{0:T(128)} %param.18) | copy-start | bytes 388
  37.9 2.3 %copy-start.16 = (f32[256]{0:T(256)S(1)}, f32[256]{0:T(256)}, u32[]{:S(2)}) copy-start(f32[256]{0:T(256)} %param.21) | copy-start | bytes 3076
  38.0 8.4 %copy-start = (bf16[256,4,4,4,32]{0,4,3,2,1:T(8,128)(2,1)S(1)}, bf16[256,4,4,4,32]{0,4,3,2,1:T(8,128)(2,1)}, u32[]{:S(2)}) copy-start(bf16[256,4,4,4,32]{0,4,3,2,1:T(8,128)(2,1)} %param.20) | copy-start | bytes 3145732
  38.0 8.4 %copy-start.1 = (bf16[256,4,4,4,32]{0,4,3,2,1:T(8,128)(2,1)S(1)}, bf16[256,4,4,4,32]{0,4,3,2,1:T(8,128)(2,1)}, u32[]{:S(2)}) copy-start(bf16[256,4,4,4,32]{0,4,3,2,1:T(8,128)(2,1)} %param.22) | copy-start | bytes 3145732
  69.0 9.2 %copy-start.5 = (f32[8]{0:T(128)S(1)}, f32[8]{0:T(128)}, u32[]{:S(2)}) copy-start(f32[8]{0:T(128)} %bias.1) | copy-start | bytes 100

commit v3 on v2

--- a/solution.py
+++ b/solution.py
@@ -113,8 +113,8 @@
             for z in range(4):
                 moved = v if z == 0 else pltpu.roll(v, 32 * z, 1)
                 at = slice(128 * i + 32 * z, 128 * i + 32 * z + 32)
-                t2[t, at, 0:128] = jnp.where(wide >= 32 * z, moved, 0.0).astype(BF)
-                t2[t, at, 128:256] = jnp.where(wide < 32 * z, moved, 0.0).astype(BF)
+                t2[at, 256 * t : 256 * t + 128] = jnp.where(wide >= 32 * z, moved, 0.0).astype(BF)
+                t2[at, 256 * t + 128 : 256 * t + 256] = jnp.where(wide < 32 * z, moved, 0.0).astype(BF)
 
     lane = iota((8, 128), 1)
 
@@ -130,7 +130,7 @@
             )
         return carry
 
-    lax.fori_loop(0, 12, windows, 0)
+    lax.fori_loop(0, 12, windows, 0, unroll=True)
 
     rows = jnp.concatenate(
         [win[p : p + 10].reshape(800, 128).astype(BF) for p in range(3)], axis=1
@@ -153,20 +153,19 @@
             hp[x, y] = jnp.concatenate([h * mask, d * mask], axis=0).astype(BF)
         return carry
 
-    lax.fori_loop(0, 10, first, 0)
-
-    for t in range(9):
-        p, q = divmod(t, 3)
-        part = lax.dot_general(
-            hp[p : p + 8, q : q + 8].reshape(1024, 256),
-            t2[t],
-            (((1,), (1,)), ((), ())),
-            preferred_element_type=F32,
+    lax.fori_loop(0, 10, first, 0, unroll=2)
+
+    for c in range(2):
+        rows = jnp.concatenate(
+            [
+                hp[4 * c + t // 3 : 4 * c + t // 3 + 4, t % 3 : t % 3 + 8].reshape(512, 256)
+                for t in range(9)
+            ],
+            axis=1,
         )
-        if t == 0:
-            acc2[...] = part
-        else:
-            acc2[...] += part
+        acc2[512 * c : 512 * c + 512] = lax.dot_general(
+            rows, t2[...], (((1,), (1,)), ((), ())), preferred_element_type=F32
+        )
 
     for x in range(8):
         for y in range(8):
@@ -372,7 +371,7 @@
             pltpu.VMEM((12, 80, 128), F32),
             pltpu.VMEM((800, 512), F32),
             pltpu.VMEM((10, 10, 16, 256), BF),
-            pltpu.VMEM((9, 256, 256), BF),
+            pltpu.VMEM((256, 2304), BF),
             pltpu.VMEM((1024, 256), F32),
             pltpu.VMEM((64, 2048), BF),
         ],

time: 80.1 us -> 78 us (0.974)
  Pallas kernels: 11.6 us -> 9.44 us
    pallas_call x1, Pallas kernels: 5.66 us -> 3.54 us  [body(): lift(tile, from_right, from_left, t1, w2, flat_lift(lift_weight), flat_li...]
  transfers between devices with their start and end apart: 4 -> 4, of which waited for: 2 -> 2; matrix products, arithmetic and copies ran while one was open for 5% -> 5% of each run, Pallas kernels for 9% -> 6%
where the time goes in v3:
time: 78 us; the launch traced here: 77.5 us
  starting transfers between devices  24.7 us (32%)
  blocking collectives  23.7 us (30%)
  waiting for transfers between devices  12.3 us (16%)
  Pallas kernels  9.44 us (12%)
  local copies, waits for them, and re-layouts  6.37 us (8%)
  between operations  0.93 us (1%)
    all_to_all x1, blocking collectives, body(): gathered = lax.all_to_all(lifted, ('sx', 'sy'), 0, 0, tiled=True)  14.5 us
    ppermute x1, starting transfers between devices, body(): from_right = lax.ppermute(to_left, 'sz', [(i + 1, i) for i in range(15)])  10.3 us
    all_to_all x1, blocking collectives, body(): mine = lax.all_to_all(parts, 'sy', 0, 0, tiled=True)  9.14 us
    all_to_all x1, starting transfers between devices, body(): near = lax.all_to_all(faces, ('sx', 'sy'), 0, 0, tiled=True)  9.07 us
    all_to_all x1, waiting for transfers between devices, body(): near = lax.all_to_all(faces, ('sx', 'sy'), 0, 0, tiled=True)  6.33 us
    ppermute x1, waiting for transfers between devices, body(): from_left = lax.ppermute(to_right, 'sz', [(i, i + 1) for i in range(15)])  6.01 us
    pallas_call x1, Pallas kernels, body(): lift(tile, from_right, from_left, t1, w2, flat_lift(lift_weight), flat_li...  3.54 us
    all_to_all x1, starting transfers between devices, body(): shares = lax.all_to_all(share, 'sx', 0, 0, tiled=True)  3.38 us
  transfers between devices with their start and end apart: 4, of which 2 were waited for; matrix products, arithmetic and copies ran while one was open for 5% of the time, Pallas kernels for 6%

profile of v3, /device:TPU:6, one launch (start us, length us, event | category | flops | bytes accessed | tf_op | source)
XLA Modules:
  0.0 77.5 jit_solution(4057050103341999615)
XLA Ops:
  0.6 0.0 copy-start.4
  0.6 0.8 %copy-done.4 = bf16[4,8,8,16]{3,2,1,0:T(8,128)(2,1)S(1)} copy-done((bf16[4,8,8,16]{3,2,1,0:T(8,128)(2,1)S(1)}, bf16[4,8,8,16]{3,2,1,0:T(8,128)(2,1)}, u32[]{:S(2)}) %copy-start.4) | copy-done | bytes 8216
  1.5 0.9 %shard_map.140 = (bf16[64,64]{1,0:T(8,128)(2,1)S(1)}, bf16[32,8,128]{2,1,0:T(8,128)(2,1)}) custom-call(bf16[4,8,8,16]{3,2,1,0:T(8,128)(2,1)S(1)} %copy-done.4), custom_call_target="tpu_custom_call" | custom-call | flops 1000000 | bytes 100000 | tf_op jit(solution)/shard_map/pallas_call | solution.py:333
  2.3 9.1 %all-to-all-start = ((bf16[32,8,128]{2,1,0:T(8,128)(2,1)}), bf16[32,8,128]{2,1,0:T(8,128)(2,1)S(1)}, u32[]{:S(2)}, u32[]{:S(2)}) async-start(bf16[32,8,128]{2,1,0:T(8,128)(2,1)} %get-tuple-element.10), calls=%async_computation | async-start | bytes 131072 | tf_op jit(solution)/shard_map/all_to_all | solution.py:339
  11.4 0.0 copy-done.12
  11.5 0.0 copy-done.13
  11.5 0.0 copy-done.2
  11.5 0.0 copy-done.3
  11.5 0.8 %shard_map.143 = bf16[4,216,128]{2,1,0:T(8,128)(2,1)} custom-call(bf16[216,256]{1,0:T(8,128)(2,1)S(1)} %bitcast.23, bf16[216,256]{1,0:T(8,128)(2,1)S(1)} %bitcast.24), custom_call_target="tpu_custom_call" | custom-call | flops 1000000 | bytes 100000 | tf_op jit(solution)/shard_map/pallas_call | solution.py:352
  12.3 0.8 fusion.3
  13.1 6.3 %all-to-all-done.slots = bf16[32,8,128]{2,1,0:T(8,128)(2,1)S(1)} async-done(((bf16[32,8,128]{2,1,0:T(8,128)(2,1)}), bf16[32,8,128]{2,1,0:T(8,128)(2,1)S(1)}, u32[]{:S(2)}, u32[]{:S(2)}) %all-to-all-start) | async-done | bytes 65568 | tf_op jit(solution)/shard_map/all_to_all | solution.py:339
  19.4 3.4 %all-to-all-start.2 = ((bf16[4,216,128]{2,1,0:T(8,128)(2,1)}), bf16[4,216,128]{2,1,0:T(8,128)(2,1)S(1)}, u32[]{:S(2)}, u32[]{:S(2)}) async-start(bf16[4,216,128]{2,1,0:T(8,128)(2,1)} %shard_map.143), calls=%async_computation.2 | async-start | bytes 442368 | tf_op jit(solution)/shard_map/all_to_all | solution.py:355
  22.8 0.0 copy-start.10
  22.8 0.8 %fusion.4 = (bf16[3,3,32,32]{3,2,1,0:T(8,128)(2,1)}, bf16[3,3,32,32]{3,2,1,0:T(8,128)(2,1)}, bf16[3,3,32,32]{3,2,1,0:T(8,128)(2,1)}, bf16[3,3,32,32]{3,2,1,0:T(8...) fusion(bf16[3,3,12,32]{3,2,1,0:T(8,128)(2,1)S(1)} %reshape.37), kind=kLoop, calls=%fused_computation.6 | loop fusion | bytes 117504 | tf_op jit(solution)/shard_map/jit(_pad)/pad | solution.py:303
  23.6 0.2 copy-done.10
  23.8 0.2 copy.17
  24.0 0.0 copy-start.11
  24.0 0.2 reshape.41
  24.2 0.8 copy-done.11
  24.9 0.2 copy.18
  25.1 0.2 reshape.42
  25.3 0.3 shard_map.141
  25.6 10.3 %collective-permute-start = (bf16[48,128]{1,0:T(8,128)(2,1)S(1)}, bf16[48,128]{1,0:T(8,128)(2,1)S(1)}, u32[]{:S(2)}, u32[]{:S(2)}) collective-permute-start(bf16[48,128]{1,0:T(8,128)(2,1)S(1)} %get-tuple-element.12), channel_id=1, source_target_pairs={{1,0},{2,1},{3,2},{4,3},{5,4},{6,5},{7,6},{8,7},{9,8},{10,9},{11,1... | collective-permute-start | bytes 36872 | tf_op jit(solution)/shard_map/ppermute | solution.py:346
  35.9 1.9 %collective-permute-start.1 = (bf16[48,128]{1,0:T(8,128)(2,1)S(1)}, bf16[48,128]{1,0:T(8,128)(2,1)S(1)}, u32[]{:S(2)}, u32[]{:S(2)}) collective-permute-start(bf16[48,128]{1,0:T(8,128)(2,1)S(1)} %get-tuple-element.13), channel_id=1, source_target_pairs={{0,1},{1,2},{2,3},{3,4},{4,5},{5,6},{6,7},{7,8},{8,9},{9,10},{10,1... | collective-permute-start | bytes 36872 | tf_op jit(solution)/shard_map/ppermute | solution.py:347
  37.9 0.0 copy-start.6
  37.9 0.0 copy-start.7
  37.9 0.0 copy-start.8
  37.9 0.0 copy-start.14
  37.9 0.0 copy-start.15
  37.9 0.0 copy-start.16
  38.0 0.0 copy-start
  38.0 0.0 copy-start.1
  38.0 0.7 copy-done.6
  38.7 0.0 copy-done.7
  38.8 0.0 copy-done.8
  38.8 0.0 copy-done.9
  38.9 1.3 %concatenate.9 = bf16[3,3,32,512]{3,2,1,0:T(8,128)(2,1)S(1)} concatenate(bf16[3,3,32,32]{3,2,1,0:T(8,128)(2,1)} %get-tuple-element.27, bf16[3,3,32,32]{3,2,1,0:T(8,128)(2,1)} %get-tuple-element.26, bf16[3,3,32,32]{3,2,1,0:T(8,128)(2,1)} %get-tuple-element.25, bf16[3,3,32,32]{3,2,1,0:T(8,128)(2,1)} %get-tuple-element.24, bf16[3,3,32,32]{3,2,1,0:T(8,128)(2,1)} %get-tuple-element.23, ...), dimensions={3} | concatenate | bytes 589824 | tf_op jit(solution)/shard_map/concatenate | solution.py:306
  40.2 0.1 concatenate.11
  40.3 0.0 collective-permute-done.right
  40.3 6.0 %collective-permute-done.1.left = bf16[48,128]{1,0:T(8,128)(2,1)S(1)} collective-permute-done((bf16[48,128]{1,0:T(8,128)(2,1)S(1)}, bf16[48,128]{1,0:T(8,128)(2,1)S(1)}, u32[]{:S(2)}, u32[]{:S(2)}) %collective-permute-start.1) | collective-permute-done | bytes 12320 | tf_op jit(solution)/shard_map/ppermute | solution.py:347
  46.3 0.0 copy-done.1
  46.3 3.5 %shard_map.142 = bf16[32,16,128]{2,1,0:T(8,128)(2,1)S(1)} custom-call(bf16[192,64]{1,0:T(8,128)(2,1)S(1)} %get-tuple-element.11.tile, bf16[48,128]{1,0:T(8,128)(2,1)S(1)} %collective-permute-done.right, bf16[48,128]{1,0:T(8,128)(2,1)S(1)} %collective-permute-done.1.left, bf16[384,512]{1,0:T(8,128)(2,1)S(1)} %bitcast.20, bf16[9,64,128]{2,1,0:T(8,128)(2,1)S(1)} %fusion.2.w2, ...), custom_call_target="tpu_custom_call" | custom-call | flops 10000000 | bytes 100000 | tf_op jit(solution)/shard_map/pallas_call | solution.py:382
  49.9 0.0 all-to-all-done.2.weights
  49.9 14.5 %all_to_all.20.got = bf16[32,16,128]{2,1,0:T(8,128)(2,1)S(1)} all-to-all(bf16[32,16,128]{2,1,0:T(8,128)(2,1)S(1)} %shard_map.142), channel_id=1, replica_groups=mesh['sx'=4,'sy'=8,'sz'=16] {'sx','sy'}, dimensions={0} | all-to-all | bytes 262144 | tf_op jit(solution)/shard_map/all_to_all | solution.py:392
  64.4 2.4 %shard_map.144 = bf16[8,16,512]{2,1,0:T(8,128)(2,1)S(1)} custom-call(bf16[32,16,128]{2,1,0:T(8,128)(2,1)S(1)} %all_to_all.20.got, bf16[4,216,128]{2,1,0:T(8,128)(2,1)S(1)} %all-to-all-done.2.weights), custom_call_target="tpu_custom_call" | custom-call | flops 10000000 | bytes 100000 | tf_op jit(solution)/shard_map/pallas_call | solution.py:393
  66.8 0.0 copy-start.5
  66.8 9.1 %all_to_all.21.got = bf16[8,16,512]{2,1,0:T(8,128)(2,1)S(1)} all-to-all(bf16[8,16,512]{2,1,0:T(8,128)(2,1)S(1)} %shard_map.144), channel_id=1, replica_groups=mesh['sx'=4,'sy'=8,'sz'=16] {'sy'}, dimensions={0} | all-to-all | bytes 262144 | tf_op jit(solution)/shard_map/all_to_all | solution.py:406
  76.0 1.5 %shard_map.145 = (bf16[8,8,4,16]{3,2,1,0:T(4,128)(2,1)}, bf16[8,8,4,16]{3,2,1,0:T(4,128)(2,1)}) custom-call(bf16[8,16,512]{2,1,0:T(8,128)(2,1)S(1)} %all_to_all.21.got, f32[8]{0:T(128)S(1)} %copy-done.5), custom_call_target="tpu_custom_call" | custom-call | flops 1000000 | bytes 100000 | tf_op jit(solution)/shard_map/pallas_call | solution.py:407
  (17 shorter events, 0.2 us)
Async XLA Ops:
  0.6 0.8 %copy-start.4 = (bf16[4,8,8,16]{3,2,1,0:T(8,128)(2,1)S(1)}, bf16[4,8,8,16]{3,2,1,0:T(8,128)(2,1)}, u32[]{:S(2)}) copy-start(bf16[4,8,8,16]{3,2,1,0:T(8,128)(2,1)} %dens.1) | copy-start | bytes 24580
  1.5 9.9 %copy-start.12 = (bf16[32,3,3,3,4]{0,4,3,2,1:T(4,128)(2,1)S(1)}, bf16[32,3,3,3,4]{0,4,3,2,1:T(4,128)(2,1)}, u32[]{:S(2)}) copy-start(bf16[32,3,3,3,4]{0,4,3,2,1:T(4,128)(2,1)} %param.16) | copy-start | bytes 20740
  1.5 10.0 %copy-start.13 = (bf16[32,3,3,3,4]{0,4,3,2,1:T(4,128)(2,1)S(1)}, bf16[32,3,3,3,4]{0,4,3,2,1:T(4,128)(2,1)}, u32[]{:S(2)}) copy-start(bf16[32,3,3,3,4]{0,4,3,2,1:T(4,128)(2,1)} %param.14) | copy-start | bytes 20740
  2.3 9.2 %copy-start.2 = (bf16[256,3,3,3,8]{0,4,3,2,1:T(8,128)(2,1)S(1)}, bf16[256,3,3,3,8]{0,4,3,2,1:T(8,128)(2,1)}, u32[]{:S(2)}) copy-start(bf16[256,3,3,3,8]{0,4,3,2,1:T(8,128)(2,1)} %param.23) | copy-start | bytes 331780
  2.3 9.2 %copy-start.3 = (bf16[256,3,3,3,8]{0,4,3,2,1:T(8,128)(2,1)S(1)}, bf16[256,3,3,3,8]{0,4,3,2,1:T(8,128)(2,1)}, u32[]{:S(2)}) copy-start(bf16[256,3,3,3,8]{0,4,3,2,1:T(8,128)(2,1)} %param.25) | copy-start | bytes 331780
  2.3 17.1 %all-to-all-start = ((bf16[32,8,128]{2,1,0:T(8,128)(2,1)}), bf16[32,8,128]{2,1,0:T(8,128)(2,1)S(1)}, u32[]{:S(2)}, u32[]{:S(2)}) async-start(bf16[32,8,128]{2,1,0:T(8,128)(2,1)} %get-tuple-element.10), calls=%async_computation | async-start | bytes 131072 | tf_op jit(solution)/shard_map/all_to_all | solution.py:339
  19.4 30.5 %all-to-all-start.2 = ((bf16[4,216,128]{2,1,0:T(8,128)(2,1)}), bf16[4,216,128]{2,1,0:T(8,128)(2,1)S(1)}, u32[]{:S(2)}, u32[]{:S(2)}) async-start(bf16[4,216,128]{2,1,0:T(8,128)(2,1)} %shard_map.143), calls=%async_computation.2 | async-start | bytes 442368 | tf_op jit(solution)/shard_map/all_to_all | solution.py:355
  22.8 1.0 %copy-start.10 = (bf16[32,3,3,3,32]{4,0,3,2,1:T(8,128)(2,1)S(1)}, bf16[32,3,3,3,32]{4,0,3,2,1:T(8,128)(2,1)}, u32[]{:S(2)}) copy-start(bf16[32,3,3,3,32]{4,0,3,2,1:T(8,128)(2,1)} %param.17) | copy-start | bytes 165892
  24.0 0.9 %copy-start.11 = (bf16[32,3,3,3,32]{4,0,3,2,1:T(8,128)(2,1)S(1)}, bf16[32,3,3,3,32]{4,0,3,2,1:T(8,128)(2,1)}, u32[]{:S(2)}) copy-start(bf16[32,3,3,3,32]{4,0,3,2,1:T(8,128)(2,1)} %param.19) | copy-start | bytes 165892
  25.6 14.7 %collective-permute-start = (bf16[48,128]{1,0:T(8,128)(2,1)S(1)}, bf16[48,128]{1,0:T(8,128)(2,1)S(1)}, u32[]{:S(2)}, u32[]{:S(2)}) collective-permute-start(bf16[48,128]{1,0:T(8,128)(2,1)S(1)} %get-tuple-element.12), channel_id=1, source_target_pairs={{1,0},{2,1},{3,2},{4,3},{5,4},{6,5},{7,6},{8,7},{9,8},{10,9},{11,1... | collective-permute-start | bytes 36872 | tf_op jit(solution)/shard_map/ppermute | solution.py:346
  35.9 10.4 %collective-permute-start.1 = (bf16[48,128]{1,0:T(8,128)(2,1)S(1)}, bf16[48,128]{1,0:T(8,128)(2,1)S(1)}, u32[]{:S(2)}, u32[]{:S(2)}) collective-permute-start(bf16[48,128]{1,0:T(8,128)(2,1)S(1)} %get-tuple-element.13), channel_id=1, source_target_pairs={{0,1},{1,2},{2,3},{3,4},{4,5},{5,6},{6,7},{7,8},{8,9},{9,10},{10,1... | collective-permute-start | bytes 36872 | tf_op jit(solution)/shard_map/ppermute | solution.py:347
  37.9 0.9 %copy-start.6 = (bf16[3,3,32,32]{3,2,1,0:T(8,128)(2,1)S(1)}, bf16[3,3,32,32]{3,2,1,0:T(8,128)(2,1)}, u32[]{:S(2)}) copy-start(bf16[3,3,32,32]{3,2,1,0:T(8,128)(2,1)} %get-tuple-element.18) | copy-start | bytes 55300
  37.9 0.9 %copy-start.7 = (bf16[3,3,32,32]{3,2,1,0:T(8,128)(2,1)S(1)}, bf16[3,3,32,32]{3,2,1,0:T(8,128)(2,1)}, u32[]{:S(2)}) copy-start(bf16[3,3,32,32]{3,2,1,0:T(8,128)(2,1)} %get-tuple-element.19) | copy-start | bytes 55300
  37.9 0.9 %copy-start.8 = (bf16[3,3,32,32]{3,2,1,0:T(8,128)(2,1)S(1)}, bf16[3,3,32,32]{3,2,1,0:T(8,128)(2,1)}, u32[]{:S(2)}) copy-start(bf16[3,3,32,32]{3,2,1,0:T(8,128)(2,1)} %get-tuple-element.20) | copy-start | bytes 55300
  37.9 1.0 %copy-start.9 = (bf16[3,3,32,32]{3,2,1,0:T(8,128)(2,1)S(1)}, bf16[3,3,32,32]{3,2,1,0:T(8,128)(2,1)}, u32[]{:S(2)}) copy-start(bf16[3,3,32,32]{3,2,1,0:T(8,128)(2,1)} %get-tuple-element.21) | copy-start | bytes 55300
  37.9 2.3 %copy-start.14 = (f32[32]{0:T(128)S(1)}, f32[32]{0:T(128)}, u32[]{:S(2)}) copy-start(f32[32]{0:T(128)} %param.15) | copy-start | bytes 388
  37.9 2.3 %copy-start.15 = (f32[32]{0:T(128)S(1)}, f32[32]{0:T(128)}, u32[]{:S(2)}) copy-start(f32[32]{0:T(128)} %param.18) | copy-start | bytes 388
  37.9 2.3 %copy-start.16 = (f32[256]{0:T(256)S(1)}, f32[256]{0:T(256)}, u32[]{:S(2)}) copy-start(f32[256]{0:T(256)} %param.21) | copy-start | bytes 3076
  38.0 8.4 %copy-start = (bf16[256,4,4,4,32]{0,4,3,2,1:T(8,128)(2,1)S(1)}, bf16[256,4,4,4,32]{0,4,3,2,1:T(8,128)(2,1)}, u32[]{:S(2)}) copy-start(bf16[256,4,4,4,32]{0,4,3,2,1:T(8,128)(2,1)} %param.20) | copy-start | bytes 3145732
  38.0 8.4 %copy-start.1 = (bf16[256,4,4,4,32]{0,4,3,2,1:T(8,128)(2,1)S(1)}, bf16[256,4,4,4,32]{0,4,3,2,1:T(8,128)(2,1)}, u32[]{:S(2)}) copy-start(bf16[256,4,4,4,32]{0,4,3,2,1:T(8,128)(2,1)} %param.22) | copy-start | bytes 3145732
  66.8 9.2 %copy-start.5 = (f32[8]{0:T(128)S(1)}, f32[8]{0:T(128)}, u32[]{:S(2)}) copy-start(f32[8]{0:T(128)} %bias.1) | copy-start | bytes 100

commit v4 on v3

--- a/solution.py
+++ b/solution.py
@@ -97,7 +97,7 @@
 
 
 def lift_kernel(
-    tile, right, left, t1, w2, lift_w, lift_p, biases, out, dens, win, acc1, hp, t2, acc2, lhs
+    tile, right, left, t1, w2, p2, lift_w, lift_p, biases, out, dens, win, acc1, hp, t2, acc2, lhs
 ):
     def unpack(ref):
         v = ref[...].astype(F32)
@@ -109,7 +109,10 @@
     wide = iota((32, 128), 1)
     for t in range(9):
         for i in range(2):
-            v = w2[t, 32 * i : 32 * i + 32].astype(F32)
+            ref = (w2, p2)[i]
+            v = jnp.concatenate(
+                [ref[3 * t + r].astype(F32) for r in range(3)] + [jnp.zeros((32, 32), F32)], axis=1
+            )
             for z in range(4):
                 moved = v if z == 0 else pltpu.roll(v, 32 * z, 1)
                 at = slice(128 * i + 32 * z, 128 * i + 32 * z + 32)
@@ -307,11 +310,8 @@
     return jnp.pad(both, ((0, 0), (0, 32), (0, 0))).reshape(384, 512)
 
 
-def second_rows(w, p):
-    def rows(v):
-        return jnp.pad(jnp.transpose(v, (1, 2, 0, 3, 4)).reshape(9, 32, 96), ((0, 0), (0, 0), (0, 32)))
-
-    return jnp.concatenate([rows(w), rows(p)], axis=1)
+def second_rows(v):
+    return jnp.transpose(v, (1, 2, 3, 0, 4)).reshape(27, 32, 32)
 
 
 def body(
@@ -354,7 +354,7 @@
     )
     shares = lax.all_to_all(share, "sx", 0, 0, tiled=True)
     t1 = first_matrix(conv1_weight, conv1_probe)
-    w2 = second_rows(conv2_weight, conv2_probe)
+    w2, p2 = second_rows(conv2_weight), second_rows(conv2_probe)
 
     biases = jnp.concatenate(
         [lift_bias] + [conv1_bias] * 6 + [jnp.zeros(64, F32)] + [conv2_bias] * 4
@@ -375,7 +375,7 @@
             pltpu.VMEM((1024, 256), F32),
             pltpu.VMEM((64, 2048), BF),
         ],
-        specs=[VM] * 8,
+        specs=[VM] * 9,
         flops=10000000,
         mib=24,
     )
@@ -385,6 +385,7 @@
         from_left,
         t1,
         w2,
+        p2,
         flat_lift(lift_weight),
         flat_lift(lift_probe),
         biases,

time: 78 us -> 77 us (0.987)
  local copies, waits for them, and re-layouts: 6.37 us -> 4.78 us
    unnamed x34 -> x24, local copies, waits for them, and re-layouts: 2.7 us -> 0.91 us
    all_to_all x1, waiting for transfers between devices: 6.33 us -> 7.13 us  [body(): near = lax.all_to_all(faces, ('sx', 'sy'), 0, 0, tiled=True)]
  transfers between devices with their start and end apart: 4 -> 4, of which waited for: 2 -> 2; matrix products, arithmetic and copies ran while one was open for 5% -> 5% of each run, Pallas kernels for 6% -> 7%
where the time goes in v4:
time: 77 us; the launch traced here: 76.5 us
  starting transfers between devices  24.7 us (32%)
  blocking collectives  23.6 us (31%)
  waiting for transfers between devices  12.4 us (16%)
  Pallas kernels  10.2 us (13%)
  local copies, waits for them, and re-layouts  4.78 us (6%)
  between operations  0.85 us (1%)
    all_to_all x1, blocking collectives, body(): gathered = lax.all_to_all(lifted, ('sx', 'sy'), 0, 0, tiled=True)  14.5 us
    ppermute x1, starting transfers between devices, body(): from_right = lax.ppermute(to_left, 'sz', [(i + 1, i) for i in range(15)])  10.3 us
    all_to_all x1, blocking collectives, body(): mine = lax.all_to_all(parts, 'sy', 0, 0, tiled=True)  9.14 us
    all_to_all x1, starting transfers between devices, body(): near = lax.all_to_all(faces, ('sx', 'sy'), 0, 0, tiled=True)  9.07 us
    all_to_all x1, waiting for transfers between devices, body(): near = lax.all_to_all(faces, ('sx', 'sy'), 0, 0, tiled=True)  7.13 us
    ppermute x1, waiting for transfers between devices, body(): from_left = lax.ppermute(to_right, 'sz', [(i, i + 1) for i in range(15)])  5.26 us
    pallas_call x1, Pallas kernels, body(): lift(tile, from_right, from_left, t1, w2, p2, flat_lift(lift_weight), fla...  4.31 us
    all_to_all x1, starting transfers between devices, body(): shares = lax.all_to_all(share, 'sx', 0, 0, tiled=True)  3.38 us
  transfers between devices with their start and end apart: 4, of which 2 were waited for; matrix products, arithmetic and copies ran while one was open for 5% of the time, Pallas kernels for 7%

profile of v4, /device:TPU:6, one launch (start us, length us, event | category | flops | bytes accessed | tf_op | source)
XLA Modules:
  0.0 76.5 jit_solution(12237432520207717693)
XLA Ops:
  0.6 0.0 copy-start.6
  0.6 0.8 %copy-done.6 = bf16[4,8,8,16]{3,2,1,0:T(8,128)(2,1)S(1)} copy-done((bf16[4,8,8,16]{3,2,1,0:T(8,128)(2,1)S(1)}, bf16[4,8,8,16]{3,2,1,0:T(8,128)(2,1)}, u32[]{:S(2)}) %copy-start.6) | copy-done | bytes 8216
  1.5 0.0 copy-start.8
  1.5 0.0 copy-start.5
  1.5 0.9 %shard_map.140 = (bf16[64,64]{1,0:T(8,128)(2,1)S(1)}, bf16[32,8,128]{2,1,0:T(8,128)(2,1)}) custom-call(bf16[4,8,8,16]{3,2,1,0:T(8,128)(2,1)S(1)} %copy-done.6), custom_call_target="tpu_custom_call" | custom-call | flops 1000000 | bytes 100000 | tf_op jit(solution)/shard_map/pallas_call | solution.py:333
  2.3 0.0 copy-start.4
  2.3 9.1 %all-to-all-start = ((bf16[32,8,128]{2,1,0:T(8,128)(2,1)}), bf16[32,8,128]{2,1,0:T(8,128)(2,1)S(1)}, u32[]{:S(2)}, u32[]{:S(2)}) async-start(bf16[32,8,128]{2,1,0:T(8,128)(2,1)} %get-tuple-element.10), calls=%async_computation | async-start | bytes 131072 | tf_op jit(solution)/shard_map/all_to_all | solution.py:339
  11.4 0.0 copy-done.8
  11.5 0.0 copy-done.5
  11.5 0.0 copy-done.4
  11.5 0.8 %shard_map.143 = bf16[4,216,128]{2,1,0:T(8,128)(2,1)} custom-call(bf16[216,256]{1,0:T(8,128)(2,1)S(1)} %bitcast.29, bf16[216,256]{1,0:T(8,128)(2,1)S(1)} %bitcast.30), custom_call_target="tpu_custom_call" | custom-call | flops 1000000 | bytes 100000 | tf_op jit(solution)/shard_map/pallas_call | solution.py:352
  12.3 7.1 %all-to-all-done.slots = bf16[32,8,128]{2,1,0:T(8,128)(2,1)S(1)} async-done(((bf16[32,8,128]{2,1,0:T(8,128)(2,1)}), bf16[32,8,128]{2,1,0:T(8,128)(2,1)S(1)}, u32[]{:S(2)}, u32[]{:S(2)}) %all-to-all-start) | async-done | bytes 65568 | tf_op jit(solution)/shard_map/all_to_all | solution.py:339
  19.4 3.4 %all-to-all-start.2 = ((bf16[4,216,128]{2,1,0:T(8,128)(2,1)}), bf16[4,216,128]{2,1,0:T(8,128)(2,1)S(1)}, u32[]{:S(2)}, u32[]{:S(2)}) async-start(bf16[4,216,128]{2,1,0:T(8,128)(2,1)} %shard_map.143), calls=%async_computation.2 | async-start | bytes 442368 | tf_op jit(solution)/shard_map/all_to_all | solution.py:355
  22.8 0.0 copy-start.9
  22.8 0.7 fusion
  23.5 0.0 copy-done.9
  23.6 0.3 shard_map.141
  23.9 10.3 %collective-permute-start = (bf16[48,128]{1,0:T(8,128)(2,1)S(1)}, bf16[48,128]{1,0:T(8,128)(2,1)S(1)}, u32[]{:S(2)}, u32[]{:S(2)}) collective-permute-start(bf16[48,128]{1,0:T(8,128)(2,1)S(1)} %get-tuple-element.12), channel_id=1, source_target_pairs={{1,0},{2,1},{3,2},{4,3},{5,4},{6,5},{7,6},{8,7},{9,8},{10,9},{11,1... | collective-permute-start | bytes 36872 | tf_op jit(solution)/shard_map/ppermute | solution.py:346
  34.2 1.9 %collective-permute-start.1 = (bf16[48,128]{1,0:T(8,128)(2,1)S(1)}, bf16[48,128]{1,0:T(8,128)(2,1)S(1)}, u32[]{:S(2)}, u32[]{:S(2)}) collective-permute-start(bf16[48,128]{1,0:T(8,128)(2,1)S(1)} %get-tuple-element.13), channel_id=1, source_target_pairs={{0,1},{1,2},{2,3},{3,4},{4,5},{5,6},{6,7},{7,8},{8,9},{9,10},{10,1... | collective-permute-start | bytes 36872 | tf_op jit(solution)/shard_map/ppermute | solution.py:347
  36.2 0.0 copy-start.10
  36.2 0.0 copy-start.11
  36.2 0.0 copy-start.2
  36.2 0.0 copy-start.3
  36.2 0.8 %fusion.1 = (bf16[3,3,32,32]{3,2,1,0:T(8,128)(2,1)}, bf16[3,3,32,32]{3,2,1,0:T(8,128)(2,1)}, bf16[3,3,32,32]{3,2,1,0:T(8,128)(2,1)}, bf16[3,3,32,32]{3,2,1,0:T(8...) fusion(bf16[3,3,12,32]{3,2,1,0:T(8,128)(2,1)S(1)} %reshape.37), kind=kLoop, calls=%fused_computation.1 | loop fusion | bytes 117504 | tf_op jit(solution)/shard_map/jit(_pad)/pad | solution.py:306
  37.0 0.0 copy-start
  37.0 0.0 copy-start.1
  37.1 1.5 %concatenate.6 = bf16[3,3,32,512]{3,2,1,0:T(8,128)(2,1)S(1)} concatenate(bf16[3,3,32,32]{3,2,1,0:T(8,128)(2,1)} %get-tuple-element.27, bf16[3,3,32,32]{3,2,1,0:T(8,128)(2,1)} %get-tuple-element.26, bf16[3,3,32,32]{3,2,1,0:T(8,128)(2,1)} %get-tuple-element.25, bf16[3,3,32,32]{3,2,1,0:T(8,128)(2,1)} %get-tuple-element.24, bf16[3,3,32,32]{3,2,1,0:T(8,128)(2,1)} %get-tuple-element.23, ...), dimensions={3} | concatenate | bytes 589824 | tf_op jit(solution)/shard_map/concatenate | solution.py:309
  38.6 0.0 copy-done.10
  38.6 0.0 copy-done.11
  38.6 0.8 concatenate.7
  39.4 0.0 collective-permute-done.right
  39.4 5.3 %collective-permute-done.1.left = bf16[48,128]{1,0:T(8,128)(2,1)S(1)} collective-permute-done((bf16[48,128]{1,0:T(8,128)(2,1)S(1)}, bf16[48,128]{1,0:T(8,128)(2,1)S(1)}, u32[]{:S(2)}, u32[]{:S(2)}) %collective-permute-start.1) | collective-permute-done | bytes 12320 | tf_op jit(solution)/shard_map/ppermute | solution.py:347
  44.7 0.0 copy-done.2
  44.7 0.0 copy-done.3
  44.7 0.0 copy-done
  44.7 0.0 copy-done.1
  44.7 4.3 %shard_map.142 = bf16[32,16,128]{2,1,0:T(8,128)(2,1)S(1)} custom-call(bf16[192,64]{1,0:T(8,128)(2,1)S(1)} %get-tuple-element.11.tile, bf16[48,128]{1,0:T(8,128)(2,1)S(1)} %collective-permute-done.right, bf16[48,128]{1,0:T(8,128)(2,1)S(1)} %collective-permute-done.1.left, bf16[384,512]{1,0:T(8,128)(2,1)S(1)} %bitcast.24, bf16[27,32,32]{2,1,0:T(8,128)(2,1)S(1)} %bitcast.27, ...), custom_call_target="tpu_custom_call" | custom-call | flops 10000000 | bytes 100000 | tf_op jit(solution)/shard_map/pallas_call | solution.py:382
  49.0 0.0 all-to-all-done.2.weights
  49.0 14.5 %all_to_all.20.got = bf16[32,16,128]{2,1,0:T(8,128)(2,1)S(1)} all-to-all(bf16[32,16,128]{2,1,0:T(8,128)(2,1)S(1)} %shard_map.142), channel_id=1, replica_groups=mesh['sx'=4,'sy'=8,'sz'=16] {'sx','sy'}, dimensions={0} | all-to-all | bytes 262144 | tf_op jit(solution)/shard_map/all_to_all | solution.py:393
  63.5 2.4 %shard_map.144 = bf16[8,16,512]{2,1,0:T(8,128)(2,1)S(1)} custom-call(bf16[32,16,128]{2,1,0:T(8,128)(2,1)S(1)} %all_to_all.20.got, bf16[4,216,128]{2,1,0:T(8,128)(2,1)S(1)} %all-to-all-done.2.weights), custom_call_target="tpu_custom_call" | custom-call | flops 10000000 | bytes 100000 | tf_op jit(solution)/shard_map/pallas_call | solution.py:394
  65.9 0.0 copy-start.7
  65.9 9.1 %all_to_all.21.got = bf16[8,16,512]{2,1,0:T(8,128)(2,1)S(1)} all-to-all(bf16[8,16,512]{2,1,0:T(8,128)(2,1)S(1)} %shard_map.144), channel_id=1, replica_groups=mesh['sx'=4,'sy'=8,'sz'=16] {'sy'}, dimensions={0} | all-to-all | bytes 262144 | tf_op jit(solution)/shard_map/all_to_all | solution.py:407
  75.1 0.0 copy-done.7
  75.1 1.5 %shard_map.145 = (bf16[8,8,4,16]{3,2,1,0:T(4,128)(2,1)}, bf16[8,8,4,16]{3,2,1,0:T(4,128)(2,1)}) custom-call(bf16[8,16,512]{2,1,0:T(8,128)(2,1)S(1)} %all_to_all.21.got, f32[8]{0:T(128)S(1)} %copy-done.7), custom_call_target="tpu_custom_call" | custom-call | flops 1000000 | bytes 100000 | tf_op jit(solution)/shard_map/pallas_call | solution.py:408
  (6 shorter events, 0.1 us)
Async XLA Ops:
  0.6 0.8 %copy-start.6 = (bf16[4,8,8,16]{3,2,1,0:T(8,128)(2,1)S(1)}, bf16[4,8,8,16]{3,2,1,0:T(8,128)(2,1)}, u32[]{:S(2)}) copy-start(bf16[4,8,8,16]{3,2,1,0:T(8,128)(2,1)} %dens.1) | copy-start | bytes 24580
  1.5 9.9 %copy-start.8 = (bf16[32,3,3,3,4]{0,4,3,2,1:T(4,128)(2,1)S(1)}, bf16[32,3,3,3,4]{0,4,3,2,1:T(4,128)(2,1)}, u32[]{:S(2)}) copy-start(bf16[32,3,3,3,4]{0,4,3,2,1:T(4,128)(2,1)} %param.16) | copy-start | bytes 20740
  1.5 10.0 %copy-start.5 = (bf16[256,3,3,3,8]{0,4,3,2,1:T(8,128)(2,1)S(1)}, bf16[256,3,3,3,8]{0,4,3,2,1:T(8,128)(2,1)}, u32[]{:S(2)}) copy-start(bf16[256,3,3,3,8]{0,4,3,2,1:T(8,128)(2,1)} %param.25) | copy-start | bytes 331780
  2.3 9.1 %copy-start.4 = (bf16[256,3,3,3,8]{0,4,3,2,1:T(8,128)(2,1)S(1)}, bf16[256,3,3,3,8]{0,4,3,2,1:T(8,128)(2,1)}, u32[]{:S(2)}) copy-start(bf16[256,3,3,3,8]{0,4,3,2,1:T(8,128)(2,1)} %param.23) | copy-start | bytes 331780
  2.3 17.1 %all-to-all-start = ((bf16[32,8,128]{2,1,0:T(8,128)(2,1)}), bf16[32,8,128]{2,1,0:T(8,128)(2,1)S(1)}, u32[]{:S(2)}, u32[]{:S(2)}) async-start(bf16[32,8,128]{2,1,0:T(8,128)(2,1)} %get-tuple-element.10), calls=%async_computation | async-start | bytes 131072 | tf_op jit(solution)/shard_map/all_to_all | solution.py:339
  19.4 29.6 %all-to-all-start.2 = ((bf16[4,216,128]{2,1,0:T(8,128)(2,1)}), bf16[4,216,128]{2,1,0:T(8,128)(2,1)S(1)}, u32[]{:S(2)}, u32[]{:S(2)}) async-start(bf16[4,216,128]{2,1,0:T(8,128)(2,1)} %shard_map.143), calls=%async_computation.2 | async-start | bytes 442368 | tf_op jit(solution)/shard_map/all_to_all | solution.py:355
  22.8 0.7 copy-start.9
  23.9 15.5 %collective-permute-start = (bf16[48,128]{1,0:T(8,128)(2,1)S(1)}, bf16[48,128]{1,0:T(8,128)(2,1)S(1)}, u32[]{:S(2)}, u32[]{:S(2)}) collective-permute-start(bf16[48,128]{1,0:T(8,128)(2,1)S(1)} %get-tuple-element.12), channel_id=1, source_target_pairs={{1,0},{2,1},{3,2},{4,3},{5,4},{6,5},{7,6},{8,7},{9,8},{10,9},{11,1... | collective-permute-start | bytes 36872 | tf_op jit(solution)/shard_map/ppermute | solution.py:346
  34.2 10.4 %collective-permute-start.1 = (bf16[48,128]{1,0:T(8,128)(2,1)S(1)}, bf16[48,128]{1,0:T(8,128)(2,1)S(1)}, u32[]{:S(2)}, u32[]{:S(2)}) collective-permute-start(bf16[48,128]{1,0:T(8,128)(2,1)S(1)} %get-tuple-element.13), channel_id=1, source_target_pairs={{0,1},{1,2},{2,3},{3,4},{4,5},{5,6},{6,7},{7,8},{8,9},{9,10},{10,1... | collective-permute-start | bytes 36872 | tf_op jit(solution)/shard_map/ppermute | solution.py:347
  36.2 2.4 %copy-start.10 = (f32[32]{0:T(128)S(1)}, f32[32]{0:T(128)}, u32[]{:S(2)}) copy-start(f32[32]{0:T(128)} %param.15) | copy-start | bytes 388
  36.2 2.4 %copy-start.11 = (f32[32]{0:T(128)S(1)}, f32[32]{0:T(128)}, u32[]{:S(2)}) copy-start(f32[32]{0:T(128)} %param.18) | copy-start | bytes 388
  36.2 8.5 %copy-start.2 = (bf16[32,3,3,3,32]{4,0,3,2,1:T(8,128)(2,1)S(1)}, bf16[32,3,3,3,32]{4,0,3,2,1:T(8,128)(2,1)}, u32[]{:S(2)}) copy-start(bf16[32,3,3,3,32]{4,0,3,2,1:T(8,128)(2,1)} %param.17) | copy-start | bytes 165892
  36.2 8.4 %copy-start.3 = (bf16[32,3,3,3,32]{4,0,3,2,1:T(8,128)(2,1)S(1)}, bf16[32,3,3,3,32]{4,0,3,2,1:T(8,128)(2,1)}, u32[]{:S(2)}) copy-start(bf16[32,3,3,3,32]{4,0,3,2,1:T(8,128)(2,1)} %param.19) | copy-start | bytes 165892
  37.0 7.6 %copy-start = (bf16[256,4,4,4,32]{0,4,3,2,1:T(8,128)(2,1)S(1)}, bf16[256,4,4,4,32]{0,4,3,2,1:T(8,128)(2,1)}, u32[]{:S(2)}) copy-start(bf16[256,4,4,4,32]{0,4,3,2,1:T(8,128)(2,1)} %param.20) | copy-start | bytes 3145732
  37.0 7.6 %copy-start.1 = (bf16[256,4,4,4,32]{0,4,3,2,1:T(8,128)(2,1)S(1)}, bf16[256,4,4,4,32]{0,4,3,2,1:T(8,128)(2,1)}, u32[]{:S(2)}) copy-start(bf16[256,4,4,4,32]{0,4,3,2,1:T(8,128)(2,1)} %param.22) | copy-start | bytes 3145732
  65.9 9.2 %copy-start.7 = (f32[8]{0:T(128)S(1)}, f32[8]{0:T(128)}, u32[]{:S(2)}) copy-start(f32[8]{0:T(128)} %bias.1) | copy-start | bytes 100
